TPU v7x, 32 devices: a whole 2x2x4 slice. The times are simulated.
32 devices in a mesh: row: 8 (over z, y), col: 4 (over x, core).
Axes of the slice: x: 2, y: 2, z: 4, core: 2. Of those that a mesh axis runs over, the one named last changes fastest.
Arguments:
- eigvecs: bfloat16 [131072, 4096], P('row', 'col'), may hold values from -6 to 6
- reflectors: bfloat16 [131072, 1024], P('row', 'col'), may hold values from -0.046875 to 0.046875
- t_factors: float32 [1024, 256], P('col'), as said below
- owners: int32 [2], replicated, may hold values from 0 to 3, as said below
- band_owner: int32 [1024, 1], P('row'), may hold values from 0 to 7; in each aligned block of 128 rows (0 to 127, 128 to 255, ...) at most 20 rows name the same one
Outputs:
- owned: bfloat16 [163840, 4096], P('row', 'col')
Inputs may be any that keep to these rules, and one draw needn't show every extreme that they name: `owners`: the 2 entries are different column indices, and one of them is the last column index. `t_factors`: each block of 256 rows is upper triangular. `band_owner`: among the 128 rows of one index of row, no owner is named more than 20 times.
All inputs are finite; a program needn't handle non-finite values.
Results may differ from a plain program's by a relative error of at most 0.015.
Values may be sent and summed in bfloat16 or wider, within the bound.
No kernel may reach another device: no remote copies, remote signals or barrier semaphores. Data moves between devices by JAX's collectives and lax.ppermute only.
A program may use at most 384 MiB of HBM per device.

v0:
```python
import jax
import jax.numpy as jnp
from jax import lax
from jax.sharding import PartitionSpec as P

contract_rows = (((0,), (0,)), ((), ()))


def broadcast(value, axis, source):
    kept = jnp.where(lax.axis_index(axis) == source, value, 0).astype(value.dtype)
    return lax.psum(kept, axis)


def fetch_panel(reflectors, t_factors, owners, which):
    return (
        broadcast(reflectors, "col", owners[which]),
        broadcast(t_factors.astype(jnp.bfloat16), "col", owners[which]).astype(t_factors.dtype),
    )


def project(panel_rows, field):
    if field.dtype == jnp.float32:
        return lax.dot_general(
            panel_rows.astype(jnp.float32),
            field,
            contract_rows,
            precision=lax.Precision.HIGHEST,
            preferred_element_type=jnp.float32,
        )
    return lax.dot_general(panel_rows, field, contract_rows, preferred_element_type=jnp.float32)


def settle(partial_value, triangle):
    products = lax.psum(partial_value.astype(jnp.bfloat16), "row").astype(jnp.float32)
    return jnp.dot(triangle, products, precision=lax.Precision.HIGHEST).astype(jnp.bfloat16)


def pack_slots(finished, slot_index, slot_total):
    block_count = finished.shape[0] // 128
    blocks = finished.reshape(block_count, 128, finished.shape[1])
    return jnp.zeros((slot_total, 128, finished.shape[1]), jnp.bfloat16).at[slot_index].set(blocks)


def body(eigvecs, reflectors, t_factors, owners, band_owner):
    field = eigvecs
    for which in range(2):
        panel_rows, triangle = fetch_panel(reflectors, t_factors, owners, which)
        update = settle(project(panel_rows, field), triangle)
        if which == 0:
            field = field.astype(jnp.float32) - jnp.dot(
                panel_rows, update, preferred_element_type=jnp.float32
            )
        else:
            base_field = field
            last_rows = panel_rows
            last_update = update
    block_count = base_field.shape[0] // 128
    local_width = base_field.shape[1]
    row_count = lax.axis_size("row")
    capacity = (5 * block_count + 4 * row_count - 1) // (4 * row_count)
    slot_total = row_count * capacity
    owner_of = band_owner[:, 0]
    position = jnp.arange(block_count, dtype=jnp.int32)
    shared = (owner_of[:, None] == owner_of[None, :]) & (position[None, :] < position[:, None])
    order_in = jnp.sum(shared.astype(jnp.int32), axis=1)
    slot_index = owner_of * capacity + order_in
    finished = (
        base_field - jnp.dot(last_rows, last_update, preferred_element_type=jnp.float32)
    ).astype(jnp.bfloat16)
    arrived = lax.all_to_all(
        pack_slots(finished, slot_index, slot_total), "row", split_axis=0, concat_axis=0, tiled=True
    )
    return arrived.reshape(slot_total * 128, local_width)


def solution(mesh):
    in_specs = (P("row", "col"), P("row", "col"), P("col", None), P(), P("row", None))
    out_specs = P("row", "col")
    return jax.shard_map(body, mesh=mesh, in_specs=in_specs, out_specs=out_specs, check_vma=False)
```

profile of v0, /device:TPU:0, one launch (start us, length us, event | category | flops | bytes accessed | tf_op | source)
XLA Modules:
  0.0 1645.3 jit_solution(16833816957001968534)
XLA Ops:
  6.5 0.0 all-reduce.9.cloned.1.call-start
  6.5 1.3 fusion.4
  9.1 9.5 broadcast_select_fusion
  18.6 1.7 broadcast_select_fusion.2
  20.3 0.0 all-reduce.9.cloned.1.call-update
  20.3 0.0 all-reduce.5.cloned.1.call-start
  20.4 295.8 %all-reduce.9.cloned.1.call-done = (bf16[16384,256]{1,0:T(8,128)(2,1)}, bf16[256,256]{1,0:T(8,128)(2,1)}, bf16[16384,256]{1,0:T(8,128)(2,1)}, bf16[256,256]{1,0:T(8,128)(2,1)}) async-done(((bf16[16384,256]{1,0:T(8,128)(2,1)}, bf16[256,256]{1,0:T(8,128)(2,1)}, bf16[16384,256]{1,0:T(8,128)(2,1)}, bf16[256,256]{1,0:T(8,128)(2,1)}), (bf16[16384,256]{1,0:T(8,128)(2,1)}, bf16[256,256]{1,0:T(8,128)(2,1)}, ...) | async-done | bytes 17039376 | tf_op jit(solution)/shard_map/psum | solution.py:11
  316.1 18.2 %convolution_convert_fusion.2 = bf16[256,1024]{1,0:T(8,128)(2,1)} fusion(bf16[16384,256]{1,0:T(8,128)(2,1)} %get-tuple-element.5, bf16[16384,1024]{1,0:T(8,128)(2,1)} %param.5), kind=kOutput, calls=%fused_computation.9 | convolution fusion | flops 8590196736 | bytes 42467328 | tf_op jit(solution)/shard_map/dot_general | solution.py:30
  334.3 0.0 all-reduce.5.cloned.1.call-update
  334.3 0.2 all-reduce.7.cloned.1.call-start
  334.6 72.6 %all-reduce.5.cloned.1.call-done = bf16[256,1024]{1,0:T(8,128)(2,1)} async-done(((bf16[256,1024]{1,0:T(8,128)(2,1)}), bf16[256,1024]{1,0:T(8,128)(2,1)}) %all-reduce.5.cloned.1.call-update) | async-done | bytes 524304 | tf_op jit(solution)/shard_map/psum | solution.py:34
  407.1 0.0 copy-done.1
  407.2 1.3 convolution_convert_fusion.1
  408.5 26.6 %fusion.5 = f32[16384,1024]{1,0:T(8,128)} fusion(bf16[16384,256]{1,0:T(8,128)(2,1)} %get-tuple-element.5, bf16[256,1024]{1,0:T(8,128)(2,1)S(1)} %convolution_convert_fusion.1), kind=kOutput, calls=%fused_computation.19 | convolution fusion | flops 8589934592 | bytes 76021760 | tf_op jit(solution)/shard_map/dot_general | solution.py:50
  435.1 45.6 %fusion.1 = bf16[256,1024]{1,0:T(8,128)(2,1)} fusion(bf16[16384,256]{1,0:T(8,128)(2,1)} %get-tuple-element.7, f32[16384,1024]{1,0:T(8,128)} %fusion.5, bf16[16384,1024]{1,0:T(8,128)(2,1)} %param.5), kind=kOutput, calls=%fused_computation.8 | convolution fusion | flops 51573424128 | bytes 109576192 | tf_op jit(solution)/shard_map/dot_general | solution.py:23
  480.7 0.0 all-reduce.7.cloned.1.call-update
  480.7 0.2 convert_reduce_fusion
  480.9 71.8 %all-reduce.7.cloned.1.call-done = bf16[256,1024]{1,0:T(8,128)(2,1)} async-done(((bf16[256,1024]{1,0:T(8,128)(2,1)}), bf16[256,1024]{1,0:T(8,128)(2,1)}) %all-reduce.7.cloned.1.call-update) | async-done | bytes 524304 | tf_op jit(solution)/shard_map/psum | solution.py:34
  552.7 1.3 convolution_convert_fusion
  554.0 46.4 %subtract_convert_fusion = bf16[16384,1024]{1,0:T(8,128)(2,1)} fusion(f32[16384,1024]{1,0:T(8,128)} %fusion.5, bf16[16384,1024]{1,0:T(8,128)(2,1)} %param.5, bf16[16384,256]{1,0:T(8,128)(2,1)} %get-tuple-element.7, bf16[256,1024]{1,0:T(8,128)(2,1)S(1)} %convolution_convert_fusion), kind=kOutput, calls=%fused_computation.1 | convolution fusion | flops 8657043456 | bytes 143130624 | tf_op jit(solution)/shard_map/dot_general | solution.py:68
  600.5 13.7 broadcast_in_dim.16
  614.2 82.9 %scatter_fusion = bf16[160,128,1024]{2,1,0:T(8,128)(2,1)} fusion(bf16[160,128,1024]{2,1,0:T(8,128)(2,1)} %broadcast_in_dim.16, s32[128]{0:T(128)S(1)} %fusion.3, bf16[128,128,1024]{2,1,0:T(8,128)(2,1)} %bitcast.23), kind=kCustom, calls=%fused_computation | custom fusion | bytes 100663808 | tf_op jit(solution)/shard_map/scatter | solution.py:41
  697.0 913.6 %all_to_all.5 = bf16[160,128,1024]{2,1,0:T(8,128)(2,1)} all-to-all(bf16[160,128,1024]{2,1,0:T(8,128)(2,1)} %scatter_fusion), channel_id=1, replica_groups=mesh['row'=8,'col'=4] {'row'}, dimensions={0} | all-to-all | bytes 83886080 | tf_op jit(solution)/shard_map/all_to_all | solution.py:70
  1610.6 28.2 %copy.14 = bf16[20480,1024]{1,0:T(8,128)(2,1)} copy(bf16[20480,1024]{1,0:T(8,128)(2,1)} %bitcast.22) | data formatting | bytes 83886080
  (6 shorter events, 0.0 us)
Async XLA Ops:
  6.5 309.6 %all-reduce.9.cloned.1.call-start = ((), (), s32[]{:S(2)}) async-start(), calls=%async_computation.3 | async-start | bytes 34078720 | tf_op jit(solution)/shard_map/psum | solution.py:11
  20.3 386.8 %all-reduce.5.cloned.1.call-start = ((), (), s32[]{:S(2)}) async-start(), calls=%async_computation.1 | async-start | bytes 1048576 | tf_op jit(solution)/shard_map/psum | solution.py:34
  316.1 91.0 %copy-start.1 = (bf16[256,256]{1,0:T(8,128)(2,1)S(1)}, bf16[256,256]{1,0:T(8,128)(2,1)}, u32[]{:S(2)}) copy-start(bf16[256,256]{1,0:T(8,128)(2,1)} %get-tuple-element.6) | copy-start | bytes 393220
  334.3 218.3 %all-reduce.7.cloned.1.call-start = ((), (), s32[]{:S(2)}) async-start(), calls=%async_computation.2 | async-start | bytes 1048576 | tf_op jit(solution)/shard_map/psum | solution.py:34
  435.1 45.6 %copy-start.2 = (s32[128,1]{0,1:T(1,128)S(1)}, s32[128,1]{0,1:T(1,128)}, u32[]{:S(2)}) copy-start(s32[128,1]{0,1:T(1,128)} %param.9) | copy-start | bytes 1540
  435.1 117.6 %copy-start = (bf16[256,256]{1,0:T(8,128)(2,1)S(1)}, bf16[256,256]{1,0:T(8,128)(2,1)}, u32[]{:S(2)}) copy-start(bf16[256,256]{1,0:T(8,128)(2,1)} %get-tuple-element.8) | copy-start | bytes 393220
Sparse Core Ops, SparseCore 0:
  20.5 295.6 all-reduce.8
  334.5 72.6 all-reduce.4
  480.8 71.8 all-reduce.6
where the time goes:
time: 1650 us
  blocking collectives  914 us (55%)
  waiting for transfers between devices  440 us (27%)
  matrix products  139 us (8%)
  local copies, waits for them, and re-layouts  126 us (8%)
    all_to_all x1, blocking collectives, body(): lax.all_to_all(pack_slots(finished, slot_index, slot_total), 'row', split...  914 us
    psum x1, waiting for transfers between devices, broadcast(): return lax.psum(kept, axis)  296 us
    psum x2, waiting for transfers between devices, settle(): lax.psum(partial_value.astype(jnp.bfloat16), 'row').astype(jnp.float32)  144 us
    scatter x1, local copies, waits for them, and re-layouts, pack_slots(): jnp.zeros((slot_total, 128, finished.shape[1]), jnp.bfloat16).at[slot_index]  82.9 us
    dot_general x1, matrix products, body(): jnp.dot(last_rows, last_update, preferred_element_type=jnp.float32)  46.4 us
    dot_general x1, matrix products, project(): lax.dot_general(panel_rows.astype(jnp.float32), field, contract_rows, pre...  45.6 us
  transfers between devices with their start and end apart: 3, of which 3 were waited for; matrix products, arithmetic and copies ran while one was open for 0% of the time, Pallas kernels for 0%

commit v1 on v0

v1 whole, which is shorter than its diff:
```python
import functools

import jax
import jax.numpy as jnp
from jax import lax
from jax.experimental import pallas as pl
from jax.experimental.pallas import tpu as pltpu
from jax.sharding import PartitionSpec as P


ROWS = 128
contract_rows = (((0,), (0,)), ((), ()))


def broadcast(value, axis, source):
    kept = jnp.where(lax.axis_index(axis) == source, value, 0).astype(value.dtype)
    return lax.psum(kept, axis)


def swap(value, row_count, distance):
    return lax.ppermute(value, "row", [(s, s ^ distance) for s in range(row_count)])


def pieces(total, size):
    return [(at, min(size, total - at)) for at in range(0, total, size)]


def gather_kernel(groups, count, block_ref, filled_ref, source, *rest):
    outs, (stage, in_sems, out_sems) = rest[:groups], rest[groups:]

    def inward(k):
        return pltpu.make_async_copy(source.at[block_ref[k]], stage.at[k], in_sems.at[k])

    def fetch(k, carry):
        @pl.when(filled_ref[k] > 0)
        def _():
            inward(k).start()

        return carry

    lax.fori_loop(0, groups * count, fetch, 0)
    for group in range(groups):

        def send(item, carry):
            k = group * count + item

            @pl.when(filled_ref[k] > 0)
            def _():
                inward(k).wait()

            @pl.when(filled_ref[k] <= 0)
            def _():
                stage[k] = jnp.zeros(stage.shape[1:], stage.dtype)

            pltpu.make_async_copy(stage.at[k], outs[group].at[item], out_sems.at[k]).start()
            return carry

        lax.fori_loop(0, count, send, 0)
    for group in range(groups):

        def drain(item, carry):
            k = group * count + item
            pltpu.make_async_copy(stage.at[k], outs[group].at[item], out_sems.at[k]).wait()
            return carry

        lax.fori_loop(0, count, drain, 0)


def gather_blocks(source, blocks, filled, groups, count):
    any_spec = pl.BlockSpec(memory_space=pl.ANY)
    smem_spec = pl.BlockSpec(memory_space=pltpu.SMEM)
    out = jax.ShapeDtypeStruct((count,) + source.shape[1:], source.dtype)
    total = groups * count
    return pl.pallas_call(
        functools.partial(gather_kernel, groups, count),
        out_shape=[out] * groups,
        in_specs=[smem_spec, smem_spec, any_spec],
        out_specs=[any_spec] * groups,
        scratch_shapes=[
            pltpu.VMEM((total,) + source.shape[1:], source.dtype),
            pltpu.SemaphoreType.DMA((total,)),
            pltpu.SemaphoreType.DMA((total,)),
        ],
        compiler_params=pltpu.CompilerParams(vmem_limit_bytes=56 * 2**20),
    )(blocks, filled, source)


def finish_kernel(groups, count, block_ref, filled_ref, base_ref, z_ref, a_ref, b_ref, y_ref, *outs):
    depth = a_ref.shape[-1]
    step = pl.program_id(0)
    value = z_ref[...].astype(jnp.float32)
    value = value - jnp.dot(a_ref[...], y_ref[:depth, :], preferred_element_type=jnp.float32)
    value = value - jnp.dot(b_ref[...], y_ref[depth:, :], preferred_element_type=jnp.float32)
    value = jnp.where(filled_ref[step] > 0, value, 0.0).astype(outs[0].dtype)
    for group in range(groups):

        @pl.when(step // count == group)
        def _():
            outs[group][...] = value


def finish_here(z, a, b, y, blocks, filled, groups, count, base=None, slot_total=None):
    width, depth = z.shape[2], a.shape[2]
    pick = lambda i, block_ref, *_: (block_ref[i], 0, 0)

    def out_spec(group):
        if base is not None:
            return pl.BlockSpec((None, ROWS, width), lambda i, block_ref, filled_ref, base_ref: (base_ref[0] + i, 0, 0))
        return pl.BlockSpec((None, ROWS, width), lambda i, *_: (jnp.clip(i - group * count, 0, count - 1), 0, 0))

    length = count if slot_total is None else slot_total
    return pl.pallas_call(
        functools.partial(finish_kernel, groups, count),
        grid_spec=pltpu.PrefetchScalarGridSpec(
            num_scalar_prefetch=3,
            grid=(groups * count,),
            in_specs=[
                pl.BlockSpec((None, ROWS, width), pick),
                pl.BlockSpec((None, ROWS, depth), pick),
                pl.BlockSpec((None, ROWS, depth), pick),
                pl.BlockSpec(y.shape, lambda i, *_: (0, 0)),
            ],
            out_specs=[out_spec(group) for group in range(groups)],
        ),
        out_shape=[jax.ShapeDtypeStruct((length, ROWS, width), z.dtype)] * groups,
    )(blocks, filled, jnp.zeros((1,), jnp.int32) if base is None else base.reshape(1), z, a, b, y)


def settle_kernel(groups, count, slot_ref, owned_ref, *refs):
    z_refs, (v_ref, y_ref, out_ref) = refs[:groups], refs[groups:]
    parts, depth = v_ref.shape[0], v_ref.shape[-1]
    for group in range(groups):

        @pl.when(pl.program_id(0) // count == group)
        def _():
            value = z_refs[group][...].astype(jnp.float32)
            for part in range(parts):
                value = value - jnp.dot(
                    v_ref[part], y_ref[part * depth : (part + 1) * depth, :], preferred_element_type=jnp.float32
                )
            out_ref[...] = value.astype(out_ref.dtype)


def settle_there(owned, z_list, v, y, first, stride, slots):
    groups, count, width = len(z_list), z_list[0].shape[0], owned.shape[2]
    parts, depth = v.shape[0], v.shape[3]

    def z_spec(group):
        return pl.BlockSpec((None, ROWS, width), lambda i, slot_ref: (jnp.clip(i - group * count, 0, count - 1), 0, 0))

    return pl.pallas_call(
        functools.partial(settle_kernel, groups, count),
        grid_spec=pltpu.PrefetchScalarGridSpec(
            num_scalar_prefetch=1,
            grid=(groups * count,),
            in_specs=[pl.BlockSpec(memory_space=pl.ANY)]
            + [z_spec(group) for group in range(groups)]
            + [
                pl.BlockSpec(
                    (parts, None, ROWS, depth),
                    lambda i, slot_ref: (0, (i // count) * stride + first + i % count, 0, 0),
                ),
                pl.BlockSpec(y.shape, lambda i, slot_ref: (0, 0)),
            ],
            out_specs=pl.BlockSpec((None, ROWS, width), lambda i, slot_ref: (slot_ref[i], 0, 0)),
        ),
        out_shape=jax.ShapeDtypeStruct(owned.shape, owned.dtype),
        input_output_aliases={1: 0},
    )(slots, owned, *z_list, v, y)


def body(eigvecs, reflectors, t_factors, owners, band_owner):
    row_count, col_count = lax.axis_size("row"), lax.axis_size("col")
    me, col = lax.axis_index("row"), lax.axis_index("col")
    block_count = eigvecs.shape[0] // ROWS
    width = eigvecs.shape[1]
    depth = reflectors.shape[1]
    capacity = (5 * block_count + 4 * row_count - 1) // (4 * row_count)
    slot_total = row_count * capacity
    early = 7 * capacity // 10
    share = 2 * depth // col_count
    half = row_count // 2
    order = list(range(half // 2, half)) + list(range(half, row_count)) + list(range(1, half // 2))
    early_parts = [(0, max(1, early // 6))]
    early_parts += [(early_parts[0][1], early - early_parts[0][1])]
    late_parts = [(early + at, count) for at, count in pieces(capacity - early, 4)]

    owner_of = band_owner[:, 0]
    position = jnp.arange(block_count, dtype=jnp.int32)
    shared = (owner_of[:, None] == owner_of[None, :]) & (position[None, :] < position[:, None])
    order_in = jnp.sum(shared.astype(jnp.int32), axis=1)
    slot_index = owner_of * capacity + order_in
    hits = (slot_index[None, :] == jnp.arange(slot_total, dtype=jnp.int32)[:, None]).astype(jnp.int32)
    slot_table = jnp.stack([jnp.sum(hits * position[None, :], axis=1), jnp.sum(hits, axis=1)])

    def tables(at, count):
        starts = [(me ^ d) * capacity + at for d in order]
        both = jnp.concatenate([lax.dynamic_slice(slot_table, (0, s), (2, count)) for s in starts], axis=1)
        return both[0], both[1]

    z = eigvecs.reshape(block_count, ROWS, width)

    raw = {}
    for at, count in early_parts:
        packed = gather_blocks(z, *tables(at, count), len(order), count)
        raw[at] = [swap(item, row_count, d) for d, item in zip(order, packed)]

    panels = [broadcast(reflectors, "col", owners[which]) for which in range(2)]
    mine = jnp.concatenate([jnp.where(col == owners[which], t_factors, 0.0) for which in range(2)], axis=0)
    triangles = lax.psum(mine, "col")

    partial_value = jnp.concatenate(
        [
            lax.dot_general(panel, eigvecs, contract_rows, preferred_element_type=jnp.float32)
            for panel in panels
        ],
        axis=0,
    )
    products = lax.psum(partial_value.astype(jnp.bfloat16), "row").astype(jnp.float32)
    gram = lax.psum(
        lax.dot_general(panels[1], panels[0], contract_rows, preferred_element_type=jnp.float32), "row"
    )
    first = jnp.dot(triangles[:depth], products[:depth], precision=lax.Precision.HIGHEST).astype(jnp.bfloat16)
    rest = products[depth:] - jnp.dot(gram, first.astype(jnp.float32), precision=lax.Precision.HIGHEST)
    second = jnp.dot(triangles[depth:], rest, precision=lax.Precision.HIGHEST).astype(jnp.bfloat16)
    update = jnp.concatenate([first, second], axis=0)

    both = jnp.concatenate(panels, axis=1)
    slim = lax.dynamic_slice(both, (0, col * share), (both.shape[0], share)).reshape(block_count, ROWS, share)
    slim_packed = gather_blocks(slim, *tables(0, early), len(order), early)
    slim_list = [swap(item, row_count, d) for d, item in zip(order, slim_packed)]

    v0 = panels[0].reshape(block_count, ROWS, depth)
    v1 = panels[1].reshape(block_count, ROWS, depth)

    late = {}
    for at, count in late_parts:
        done = finish_here(z, v0, v1, update, *tables(at, count), len(order), count)
        late[at] = [swap(item, row_count, d) for d, item in zip(order, done)]

    slim_list, _ = lax.optimization_barrier((slim_list, done))
    wide_there = lax.all_gather(jnp.concatenate(slim_list, axis=0), "col", axis=0)

    mine = lax.dynamic_slice(slot_table, (0, me * capacity), (2, capacity))
    (owned,) = finish_here(z, v0, v1, update, mine[0], mine[1], 1, capacity, me * capacity, slot_total)
    for at, count in early_parts:
        slots = jnp.concatenate([(me ^ d) * capacity + at + jnp.arange(count, dtype=jnp.int32) for d in order])
        owned = settle_there(owned, raw[at], wide_there, update, at, early, slots)
    for at, count in late_parts:
        for d, item in zip(order, late[at]):
            owned = lax.dynamic_update_slice(owned, item, ((me ^ d) * capacity + at, 0, 0))
    return owned.reshape(slot_total * ROWS, width)


def solution(mesh):
    in_specs = (P("row", "col"), P("row", "col"), P("col", None), P(), P("row", None))
    out_specs = P("row", "col")
    return jax.shard_map(body, mesh=mesh, in_specs=in_specs, out_specs=out_specs, check_vma=False)
```

time: 1650 us -> 1670 us (1.012); the launches traced: 1650 us -> 1650 us
  blocking collectives: 914 us -> 0 us
  waiting for transfers between devices: 440 us -> 932 us
  starting transfers between devices: 0.27 us -> 434 us
  Pallas kernels: 0 us -> 162 us
  local copies, waits for them, and re-layouts: 126 us -> 35.8 us
  matrix products: 139 us -> 49.8 us
    all_to_all x1 -> x0, blocking collectives: 914 us -> none  [body(): lax.all_to_all(pack_slots(finished, slot_index, slot_total), 'row', split...]
    ppermute x0 -> x35, waiting for transfers between devices: none -> 466 us  [swap(): lax.ppermute(value, 'row', [(s, s ^ distance) for s in range(row_count)])]
    ppermute x0 -> x35, starting transfers between devices: none -> 434 us  [swap(): lax.ppermute(value, 'row', [(s, s ^ distance) for s in range(row_count)])]
    pallas_call x0 -> x8, Pallas kernels: none -> 162 us  [the longest x2 82 us: settle_there(): pl.pallas_call(functools.partial(settle_kernel, groups, count), grid_spec...]
    dot_general x6, matrix products: 139 us -> 49.8 us  [the longest x2 35.3 us: body(): lax.dot_general(panel, eigvecs, contract_rows, preferred_element_type=jnp...]
    scatter x1 -> x0, local copies, waits for them, and re-layouts: 82.9 us -> none  [pack_slots(): jnp.zeros((slot_total, 128, finished.shape[1]), jnp.bfloat16).at[slot_index]]
    psum x2 -> x3, waiting for transfers between devices: 144 us -> 178 us  [the longest x1 104 us: body(): lax.psum(partial_value.astype(jnp.bfloat16), 'row').astype(jnp.float32)]
    dynamic_update_slice x0 -> x14, local copies, waits for them, and re-layouts: none -> 18 us  [body(): lax.dynamic_update_slice(owned, item, ((me ^ d) * capacity + at, 0, 0))]
  transfers between devices with their start and end apart: 3 -> 40, of which waited for: 3 -> 10; matrix products, arithmetic and copies ran while one was open for 0% -> 5% of each run, Pallas kernels for 0% -> 10%
where the time goes in v1:
time: 1670 us; the launch traced here: 1650 us
  waiting for transfers between devices  932 us (56%)
  starting transfers between devices  434 us (26%)
  Pallas kernels  162 us (10%)
  matrix products  49.8 us (3%)
  local copies, waits for them, and re-layouts  35.8 us (2%)
  other arithmetic  18.8 us (1%)
    ppermute x35, waiting for transfers between devices, swap(): lax.ppermute(value, 'row', [(s, s ^ distance) for s in range(row_count)])  466 us
    ppermute x35, starting transfers between devices, swap(): lax.ppermute(value, 'row', [(s, s ^ distance) for s in range(row_count)])  434 us
    psum x1, waiting for transfers between devices, broadcast(): return lax.psum(kept, axis)  287 us
    psum x1, waiting for transfers between devices, body(): lax.psum(partial_value.astype(jnp.bfloat16), 'row').astype(jnp.float32)  104 us
    pallas_call x2, Pallas kernels, settle_there(): pl.pallas_call(functools.partial(settle_kernel, groups, count), grid_spec...  82 us
    psum x1, waiting for transfers between devices, body(): lax.psum(lax.dot_general(panels[1], panels[0], contract_rows, preferred_e...  74.6 us
    pallas_call x3, Pallas kernels, finish_here(): pl.pallas_call(functools.partial(finish_kernel, groups, count), grid_spec...  50.4 us
    dot_general x2, matrix products, body(): lax.dot_general(panel, eigvecs, contract_rows, preferred_element_type=jnp...  35.3 us
  transfers between devices with their start and end apart: 40, of which 10 were waited for; matrix products, arithmetic and copies ran while one was open for 5% of the time, Pallas kernels for 10%

profile of v1, /device:TPU:0, one launch (start us, length us, event | category | flops | bytes accessed | tf_op | source)
XLA Modules:
  0.0 1646.7 jit_solution(877075486475632414)
XLA Ops:
  22.5 287.4 %all-reduce.12.cloned.1.call-done = (bf16[16384,256]{1,0:T(8,128)(2,1)}, bf16[16384,256]{1,0:T(8,128)(2,1)}) async-done(((bf16[16384,256]{1,0:T(8,128)(2,1)}, bf16[16384,256]{1,0:T(8,128)(2,1)}), (bf16[16384,256]{1,0:T(8,128)(2,1)}, bf16[16384,256]{1,0:T(8,128)(2,1)})) %all-reduce.12.cloned.1.call-update) | async-done | bytes 16777232 | tf_op jit(solution)/shard_map/psum | solution.py:17
  309.9 17.6 %convolution_convert_fusion.3 = bf16[256,1024]{1,0:T(8,128)(2,1)S(1)} fusion(bf16[16384,256]{1,0:T(8,128)(2,1)} %get-tuple-element.91, bf16[16384,1024]{1,0:T(8,128)(2,1)} %param.5), kind=kOutput, calls=%fused_computation.9 | convolution fusion | flops 8590196736 | bytes 42467328 | tf_op jit(solution)/shard_map/dot_general | solution.py:214
  327.5 17.7 %convolution_convert_fusion.2 = bf16[256,1024]{1,0:T(8,128)(2,1)S(1)} fusion(bf16[16384,256]{1,0:T(8,128)(2,1)} %get-tuple-element.92, bf16[16384,1024]{1,0:T(8,128)(2,1)} %param.5), kind=kOutput, calls=%fused_computation.8 | convolution fusion | flops 8590196736 | bytes 42467328 | tf_op jit(solution)/shard_map/dot_general | solution.py:214
  375.9 103.8 %all-reduce.8.cloned.1.call-done = bf16[512,1024]{1,0:T(8,128)(2,1)} async-done(((bf16[512,1024]{1,0:T(8,128)(2,1)}), bf16[512,1024]{1,0:T(8,128)(2,1)}) %all-reduce.8.cloned.1.call-update) | async-done | bytes 1048592 | tf_op jit(solution)/shard_map/psum | solution.py:219
  485.1 74.6 %all-reduce.10.cloned.1.call-done = f32[256,256]{1,0:T(8,128)} async-done(((f32[256,256]{1,0:T(8,128)}), f32[256,256]{1,0:T(8,128)}) %all-reduce.10.cloned.1.call-update) | async-done | bytes 262160 | tf_op jit(solution)/shard_map/psum | solution.py:220
  564.4 12.6 shard_map.58
  588.7 18.6 %shard_map.60 = (bf16[12,128,1024]{2,1,0:T(8,128)(2,1)}, bf16[12,128,1024]{2,1,0:T(8,128)(2,1)}, bf16[12,128,1024]{2,1,0:T(8,128)(2,1)}, bf16[12,128,1024]{2,1,0...) custom-call(s32[84]{0:T(128)} %get-tuple-element.132.block_ref, ...), custom_call_target="tpu_custom_call" | custom-call | tf_op jit(solution)/shard_map/pallas_call | solution.py:74
  618.9 152.4 %collective-permute-done.refs_0_ = bf16[2,128,1024]{2,1,0:T(8,128)(2,1)S(1)} collective-permute-done((bf16[2,128,1024]{2,1,0:T(8,128)(2,1)}, bf16[2,128,1024]{2,1,0:T(8,128)(2,1)S(1)}, u32[]{:S(2)}, u32[]{:S(2)}) %collective-permute-start) | collective-permute-done | bytes 524320 | tf_op jit(solution)/shard_map/ppermute | solution.py:21
  783.8 73.0 %collective-permute-done.3.refs_3_ = bf16[2,128,1024]{2,1,0:T(8,128)(2,1)S(1)} collective-permute-done((bf16[2,128,1024]{2,1,0:T(8,128)(2,1)}, bf16[2,128,1024]{2,1,0:T(8,128)(2,1)S(1)}, u32[]{:S(2)}, u32[]{:S(2)}) %collective-permute-start.3) | collective-permute-done | bytes 524320 | tf_op jit(solution)/shard_map/ppermute | solution.py:21
  857.4 55.9 %collective-permute-start.17 = (bf16[12,128,1024]{2,1,0:T(8,128)(2,1)}, bf16[12,128,1024]{2,1,0:T(8,128)(2,1)}, u32[]{:S(2)}, u32[]{:S(2)}) collective-permute-start(bf16[12,128,1024]{2,1,0:T(8,128)(2,1)} %get-tuple-element.78), channel_id=1, source_target_pairs={{0,20},{4,16},{8,28},{12,24},{16,4},{20,0},{24,12},{28,8},{1,21},{... | collective-permute-start | bytes 9437192 | tf_op jit(solution)/shard_map/ppermute | solution.py:21
  913.3 103.7 %collective-permute-start.18 = (bf16[12,128,1024]{2,1,0:T(8,128)(2,1)}, bf16[12,128,1024]{2,1,0:T(8,128)(2,1)}, u32[]{:S(2)}, u32[]{:S(2)}) collective-permute-start(bf16[12,128,1024]{2,1,0:T(8,128)(2,1)} %get-tuple-element.79), channel_id=1, source_target_pairs={{0,24},{4,28},{8,16},{12,20},{16,8},{20,12},{24,0},{28,4},{1,25},{... | collective-permute-start | bytes 9437192 | tf_op jit(solution)/shard_map/ppermute | solution.py:21
  1019.7 23.1 %shard_map.62 = (bf16[4,128,1024]{2,1,0:T(8,128)(2,1)}, bf16[4,128,1024]{2,1,0:T(8,128)(2,1)}, bf16[4,128,1024]{2,1,0:T(8,128)(2,1)}, bf16[4,128,1024]{2,1,0:T(8...) custom-call(s32[28]{0:T(128)} %get-tuple-element.130.block_ref, ...), custom_call_target="tpu_custom_call" | custom-call | tf_op jit(solution)/shard_map/pallas_call | solution.py:112
  1042.8 139.2 %collective-permute-done.16.refs_2_ = bf16[12,128,1024]{2,1,0:T(8,128)(2,1)} collective-permute-done((bf16[12,128,1024]{2,1,0:T(8,128)(2,1)}, bf16[12,128,1024]{2,1,0:T(8,128)(2,1)}, u32[]{:S(2)}, u32[]{:S(2)}) %collective-permute-start.16) | collective-permute-done | bytes 3145760 | tf_op jit(solution)/shard_map/ppermute | solution.py:21
  1182.0 68.3 %collective-permute-done.17.refs_3_ = bf16[12,128,1024]{2,1,0:T(8,128)(2,1)} collective-permute-done((bf16[12,128,1024]{2,1,0:T(8,128)(2,1)}, bf16[12,128,1024]{2,1,0:T(8,128)(2,1)}, u32[]{:S(2)}, u32[]{:S(2)}) %collective-permute-start.17) | collective-permute-done | bytes 3145760 | tf_op jit(solution)/shard_map/ppermute | solution.py:21
  1250.3 77.2 %collective-permute-start.23 = (bf16[4,128,1024]{2,1,0:T(8,128)(2,1)}, bf16[4,128,1024]{2,1,0:T(8,128)(2,1)S(1)}, u32[]{:S(2)}, u32[]{:S(2)}) collective-permute-start(bf16[4,128,1024]{2,1,0:T(8,128)(2,1)} %get-tuple-element.84), channel_id=1, source_target_pairs={{0,16},{4,20},{8,24},{12,28},{16,0},{20,4},{24,8},{28,12},{1,17},{... | collective-permute-start | bytes 3145736 | tf_op jit(solution)/shard_map/ppermute | solution.py:21
  1327.5 80.4 %collective-permute-start.24 = (bf16[4,128,1024]{2,1,0:T(8,128)(2,1)}, bf16[4,128,1024]{2,1,0:T(8,128)(2,1)}, u32[]{:S(2)}, u32[]{:S(2)}) collective-permute-start(bf16[4,128,1024]{2,1,0:T(8,128)(2,1)} %get-tuple-element.85), channel_id=1, source_target_pairs={{0,20},{4,16},{8,28},{12,24},{16,4},{20,0},{24,12},{28,8},{1,21},{... | collective-permute-start | bytes 3145736 | tf_op jit(solution)/shard_map/ppermute | solution.py:21
  1407.9 36.3 %collective-permute-start.25 = (bf16[4,128,1024]{2,1,0:T(8,128)(2,1)}, bf16[4,128,1024]{2,1,0:T(8,128)(2,1)}, u32[]{:S(2)}, u32[]{:S(2)}) collective-permute-start(bf16[4,128,1024]{2,1,0:T(8,128)(2,1)} %get-tuple-element.86), channel_id=1, source_target_pairs={{0,24},{4,28},{8,16},{12,20},{16,8},{20,12},{24,0},{28,4},{1,25},{... | collective-permute-start | bytes 3145736 | tf_op jit(solution)/shard_map/ppermute | solution.py:21
  1447.7 14.8 shard_map.55.owned_ref
  1462.4 13.7 shard_map.59.owned_ref
  1476.1 68.3 %shard_map.61 = bf16[160,128,1024]{2,1,0:T(8,128)(2,1)} custom-call(s32[84]{0:T(128)} %concatenate.37.slot_ref, bf16[160,128,1024]{2,1,0:T(8,128)(2,1)} %shard_map.59.owned_ref, bf16[12,128,1024]{2,1,0:T(8,128)(2,1)} %copy-done.1, bf16[12,128,1024]{2,1,0:T(8,128)(2,1)} %collective-permute-done.15.refs_1_, ...), custom_call_target="tpu_custom_call", output_to_operand_aliasing={{}: (1, {})} | custom-call | tf_op jit(solution)/shard_map/pallas_call | solution.py:151
  1557.7 22.6 %collective-permute-start.31 = (bf16[2,128,1024]{2,1,0:T(8,128)(2,1)S(1)}, bf16[2,128,1024]{2,1,0:T(8,128)(2,1)S(1)}, u32[]{:S(2)}, u32[]{:S(2)}) collective-permute-start(bf16[2,128,1024]{2,1,0:T(8,128)(2,1)S(1)} %copy-done.19), channel_id=1, source_target_pairs={{0,20},{4,16},{8,28},{12,24},{16,4},{20,0},{24,12},{28,8},{1,21},{... | collective-permute-start | bytes 1572872 | tf_op jit(solution)/shard_map/ppermute | solution.py:21
  1582.6 21.1 %collective-permute-start.32 = (bf16[2,128,1024]{2,1,0:T(8,128)(2,1)S(1)}, bf16[2,128,1024]{2,1,0:T(8,128)(2,1)S(1)}, u32[]{:S(2)}, u32[]{:S(2)}) collective-permute-start(bf16[2,128,1024]{2,1,0:T(8,128)(2,1)S(1)} %copy-done.18), channel_id=1, source_target_pairs={{0,24},{4,28},{8,16},{12,20},{16,8},{20,12},{24,0},{28,4},{1,25},{... | collective-permute-start | bytes 1572872 | tf_op jit(solution)/shard_map/ppermute | solution.py:21
  1609.1 16.5 %collective-permute-done.30 = bf16[2,128,1024]{2,1,0:T(8,128)(2,1)S(1)} collective-permute-done((bf16[2,128,1024]{2,1,0:T(8,128)(2,1)S(1)}, bf16[2,128,1024]{2,1,0:T(8,128)(2,1)S(1)}, u32[]{:S(2)}, u32[]{:S(2)}) %collective-permute-start.30) | collective-permute-done | bytes 524320 | tf_op jit(solution)/shard_map/ppermute | solution.py:21
  1626.5 10.4 collective-permute-done.31
  (186 shorter events, 122.7 us)
Async XLA Ops:
  6.5 303.4 %all-reduce.12.cloned.1.call-start = ((), (), s32[]{:S(2)}) async-start(), calls=%async_computation.4 | async-start | bytes 33554432 | tf_op jit(solution)/shard_map/psum | solution.py:17
  18.7 357.2 %all-reduce.6.cloned.1.call-start = ((), (), s32[]{:S(2)}) async-start(), calls=%async_computation | async-start | bytes 1048576 | tf_op jit(solution)/shard_map/psum | solution.py:210
  20.5 459.2 %all-reduce.8.cloned.1.call-start = ((), (), s32[]{:S(2)}) async-start(), calls=%async_computation.1 | async-start | bytes 2097152 | tf_op jit(solution)/shard_map/psum | solution.py:219
  360.0 199.7 %all-reduce.10.cloned.1.call-start = ((), (), s32[]{:S(2)}) async-start(), calls=%async_computation.2 | async-start | bytes 524288 | tf_op jit(solution)/shard_map/psum | solution.py:220
  369.1 1093.3 %all-gather.3.cloned.1.call-start = ((), (), s32[]{:S(2)}) async-start(), calls=%async_computation.3 | async-start | bytes 16056320 | tf_op jit(solution)/shard_map/all_gather | solution.py:242
  369.9 207.1 %collective-permute-start.9 = (bf16[14,128,128]{2,1,0:T(8,128)(2,1)}, bf16[14,128,128]{2,1,0:T(8,128)(2,1)S(1)}, u32[]{:S(2)}, u32[]{:S(2)}) collective-permute-start(bf16[14,128,128]{2,1,0:T(8,128)(2,1)} %get-tuple-element.56), channel_id=1, source_target_pairs={{0,16},{4,20},{8,24},{12,28},{16,0},{20,4},{24,8},{28,12},{1,17},{... | collective-permute-start | bytes 1376264 | tf_op jit(solution)/shard_map/ppermute | solution.py:21
  372.3 204.8 %collective-permute-start.10 = (bf16[14,128,128]{2,1,0:T(8,128)(2,1)}, bf16[14,128,128]{2,1,0:T(8,128)(2,1)S(1)}, u32[]{:S(2)}, u32[]{:S(2)}) collective-permute-start(bf16[14,128,128]{2,1,0:T(8,128)(2,1)} %get-tuple-element.57), channel_id=1, source_target_pairs={{0,20},{4,16},{8,28},{12,24},{16,4},{20,0},{24,12},{28,8},{1,21},{... | collective-permute-start | bytes 1376264 | tf_op jit(solution)/shard_map/ppermute | solution.py:21
  372.6 204.5 %collective-permute-start.11 = (bf16[14,128,128]{2,1,0:T(8,128)(2,1)}, bf16[14,128,128]{2,1,0:T(8,128)(2,1)S(1)}, u32[]{:S(2)}, u32[]{:S(2)}) collective-permute-start(bf16[14,128,128]{2,1,0:T(8,128)(2,1)} %get-tuple-element.58), channel_id=1, source_target_pairs={{0,24},{4,28},{8,16},{12,20},{16,8},{20,12},{24,0},{28,4},{1,25},{... | collective-permute-start | bytes 1376264 | tf_op jit(solution)/shard_map/ppermute | solution.py:21
  607.3 409.7 %collective-permute-start.14 = (bf16[12,128,1024]{2,1,0:T(8,128)(2,1)}, bf16[12,128,1024]{2,1,0:T(8,128)(2,1)S(1)}, u32[]{:S(2)}, u32[]{:S(2)}) collective-permute-start(bf16[12,128,1024]{2,1,0:T(8,128)(2,1)} %get-tuple-element.75), channel_id=1, source_target_pairs={{0,8},{4,12},{8,0},{12,4},{16,24},{20,28},{24,16},{28,20},{1,9},{5... | collective-permute-start | bytes 9437192 | tf_op jit(solution)/shard_map/ppermute | solution.py:21
  607.4 410.1 %collective-permute-start.15 = (bf16[12,128,1024]{2,1,0:T(8,128)(2,1)}, bf16[12,128,1024]{2,1,0:T(8,128)(2,1)}, u32[]{:S(2)}, u32[]{:S(2)}) collective-permute-start(bf16[12,128,1024]{2,1,0:T(8,128)(2,1)} %get-tuple-element.76), channel_id=1, source_target_pairs={{0,12},{4,8},{8,4},{12,0},{16,28},{20,24},{24,20},{28,16},{1,13},{... | collective-permute-start | bytes 9437192 | tf_op jit(solution)/shard_map/ppermute | solution.py:21
  613.4 157.8 %collective-permute-start = (bf16[2,128,1024]{2,1,0:T(8,128)(2,1)}, bf16[2,128,1024]{2,1,0:T(8,128)(2,1)S(1)}, u32[]{:S(2)}, u32[]{:S(2)}) collective-permute-start(bf16[2,128,1024]{2,1,0:T(8,128)(2,1)} %get-tuple-element.47), channel_id=1, source_target_pairs={{0,8},{4,12},{8,0},{12,4},{16,24},{20,28},{24,16},{28,20},{1,9},{5... | collective-permute-start | bytes 1572872 | tf_op jit(solution)/shard_map/ppermute | solution.py:21
  615.0 162.4 %collective-permute-start.1 = (bf16[2,128,1024]{2,1,0:T(8,128)(2,1)}, bf16[2,128,1024]{2,1,0:T(8,128)(2,1)S(1)}, u32[]{:S(2)}, u32[]{:S(2)}) collective-permute-start(bf16[2,128,1024]{2,1,0:T(8,128)(2,1)} %get-tuple-element.48), channel_id=1, source_target_pairs={{0,12},{4,8},{8,4},{12,0},{16,28},{20,24},{24,20},{28,16},{1,13},{... | collective-permute-start | bytes 1572872 | tf_op jit(solution)/shard_map/ppermute | solution.py:21
  617.0 163.1 %collective-permute-start.2 = (bf16[2,128,1024]{2,1,0:T(8,128)(2,1)}, bf16[2,128,1024]{2,1,0:T(8,128)(2,1)S(1)}, u32[]{:S(2)}, u32[]{:S(2)}) collective-permute-start(bf16[2,128,1024]{2,1,0:T(8,128)(2,1)} %get-tuple-element.49), channel_id=1, source_target_pairs={{0,16},{4,20},{8,24},{12,28},{16,0},{20,4},{24,8},{28,12},{1,17},{... | collective-permute-start | bytes 1572872 | tf_op jit(solution)/shard_map/ppermute | solution.py:21
  856.8 325.1 %collective-permute-start.16 = (bf16[12,128,1024]{2,1,0:T(8,128)(2,1)}, bf16[12,128,1024]{2,1,0:T(8,128)(2,1)}, u32[]{:S(2)}, u32[]{:S(2)}) collective-permute-start(bf16[12,128,1024]{2,1,0:T(8,128)(2,1)} %get-tuple-element.77), channel_id=1, source_target_pairs={{0,16},{4,20},{8,24},{12,28},{16,0},{20,4},{24,8},{28,12},{1,17},{... | collective-permute-start | bytes 9437192 | tf_op jit(solution)/shard_map/ppermute | solution.py:21
  857.4 392.8 %collective-permute-start.17 = (bf16[12,128,1024]{2,1,0:T(8,128)(2,1)}, bf16[12,128,1024]{2,1,0:T(8,128)(2,1)}, u32[]{:S(2)}, u32[]{:S(2)}) collective-permute-start(bf16[12,128,1024]{2,1,0:T(8,128)(2,1)} %get-tuple-element.78), channel_id=1, source_target_pairs={{0,20},{4,16},{8,28},{12,24},{16,4},{20,0},{24,12},{28,8},{1,21},{... | collective-permute-start | bytes 9437192 | tf_op jit(solution)/shard_map/ppermute | solution.py:21
  913.3 337.0 %collective-permute-start.18 = (bf16[12,128,1024]{2,1,0:T(8,128)(2,1)}, bf16[12,128,1024]{2,1,0:T(8,128)(2,1)}, u32[]{:S(2)}, u32[]{:S(2)}) collective-permute-start(bf16[12,128,1024]{2,1,0:T(8,128)(2,1)} %get-tuple-element.79), channel_id=1, source_target_pairs={{0,24},{4,28},{8,16},{12,20},{16,8},{20,12},{24,0},{28,4},{1,25},{... | collective-permute-start | bytes 9437192 | tf_op jit(solution)/shard_map/ppermute | solution.py:21
  1017.1 310.4 %collective-permute-start.19 = (bf16[12,128,1024]{2,1,0:T(8,128)(2,1)}, bf16[12,128,1024]{2,1,0:T(8,128)(2,1)}, u32[]{:S(2)}, u32[]{:S(2)}) collective-permute-start(bf16[12,128,1024]{2,1,0:T(8,128)(2,1)} %get-tuple-element.80), channel_id=1, source_target_pairs={{0,28},{4,24},{8,20},{12,16},{16,12},{20,8},{24,4},{28,0},{1,29},{... | collective-permute-start | bytes 9437192 | tf_op jit(solution)/shard_map/ppermute | solution.py:21
  1017.6 390.3 %collective-permute-start.20 = (bf16[12,128,1024]{2,1,0:T(8,128)(2,1)}, bf16[12,128,1024]{2,1,0:T(8,128)(2,1)}, u32[]{:S(2)}, u32[]{:S(2)}) collective-permute-start(bf16[12,128,1024]{2,1,0:T(8,128)(2,1)} %get-tuple-element.81), channel_id=1, source_target_pairs={{0,4},{4,0},{8,12},{12,8},{16,20},{20,16},{24,28},{28,24},{1,5},{5... | collective-permute-start | bytes 9437192 | tf_op jit(solution)/shard_map/ppermute | solution.py:21
  1182.0 262.2 %collective-permute-start.21 = (bf16[4,128,1024]{2,1,0:T(8,128)(2,1)}, bf16[4,128,1024]{2,1,0:T(8,128)(2,1)S(1)}, u32[]{:S(2)}, u32[]{:S(2)}) collective-permute-start(bf16[4,128,1024]{2,1,0:T(8,128)(2,1)} %get-tuple-element.82), channel_id=1, source_target_pairs={{0,8},{4,12},{8,0},{12,4},{16,24},{20,28},{24,16},{28,20},{1,9},{5... | collective-permute-start | bytes 3145736 | tf_op jit(solution)/shard_map/ppermute | solution.py:21
  1250.3 195.6 %collective-permute-start.22 = (bf16[4,128,1024]{2,1,0:T(8,128)(2,1)}, bf16[4,128,1024]{2,1,0:T(8,128)(2,1)S(1)}, u32[]{:S(2)}, u32[]{:S(2)}) collective-permute-start(bf16[4,128,1024]{2,1,0:T(8,128)(2,1)} %get-tuple-element.83), channel_id=1, source_target_pairs={{0,12},{4,8},{8,4},{12,0},{16,28},{20,24},{24,20},{28,16},{1,13},{... | collective-permute-start | bytes 3145736 | tf_op jit(solution)/shard_map/ppermute | solution.py:21
  1250.3 296.2 %collective-permute-start.23 = (bf16[4,128,1024]{2,1,0:T(8,128)(2,1)}, bf16[4,128,1024]{2,1,0:T(8,128)(2,1)S(1)}, u32[]{:S(2)}, u32[]{:S(2)}) collective-permute-start(bf16[4,128,1024]{2,1,0:T(8,128)(2,1)} %get-tuple-element.84), channel_id=1, source_target_pairs={{0,16},{4,20},{8,24},{12,28},{16,0},{20,4},{24,8},{28,12},{1,17},{... | collective-permute-start | bytes 3145736 | tf_op jit(solution)/shard_map/ppermute | solution.py:21
  1327.5 220.4 %collective-permute-start.24 = (bf16[4,128,1024]{2,1,0:T(8,128)(2,1)}, bf16[4,128,1024]{2,1,0:T(8,128)(2,1)}, u32[]{:S(2)}, u32[]{:S(2)}) collective-permute-start(bf16[4,128,1024]{2,1,0:T(8,128)(2,1)} %get-tuple-element.85), channel_id=1, source_target_pairs={{0,20},{4,16},{8,28},{12,24},{16,4},{20,0},{24,12},{28,8},{1,21},{... | collective-permute-start | bytes 3145736 | tf_op jit(solution)/shard_map/ppermute | solution.py:21
  1407.9 146.4 %collective-permute-start.25 = (bf16[4,128,1024]{2,1,0:T(8,128)(2,1)}, bf16[4,128,1024]{2,1,0:T(8,128)(2,1)}, u32[]{:S(2)}, u32[]{:S(2)}) collective-permute-start(bf16[4,128,1024]{2,1,0:T(8,128)(2,1)} %get-tuple-element.86), channel_id=1, source_target_pairs={{0,24},{4,28},{8,16},{12,20},{16,8},{20,12},{24,0},{28,4},{1,25},{... | collective-permute-start | bytes 3145736 | tf_op jit(solution)/shard_map/ppermute | solution.py:21
  1445.9 136.7 %collective-permute-start.27 = (bf16[4,128,1024]{2,1,0:T(8,128)(2,1)}, bf16[4,128,1024]{2,1,0:T(8,128)(2,1)}, u32[]{:S(2)}, u32[]{:S(2)}) collective-permute-start(bf16[4,128,1024]{2,1,0:T(8,128)(2,1)} %get-tuple-element.88), channel_id=1, source_target_pairs={{0,4},{4,0},{8,12},{12,8},{16,20},{20,16},{24,28},{28,24},{1,5},{5... | collective-permute-start | bytes 3145736 | tf_op jit(solution)/shard_map/ppermute | solution.py:21
  (38 other events, 2959.2 us)
Sparse Core Ops, SparseCore 0:
  18.8 291.0 all-reduce.11
  312.2 33.4 all-reduce.5
  360.1 119.5 all-reduce.7
  482.9 76.7 all-reduce.9
  587.7 83.4 all-gather.2

commit v2 on v1

--- a/solution.py
+++ b/solution.py
@@ -10,11 +10,6 @@
 
 ROWS = 128
 contract_rows = (((0,), (0,)), ((), ()))
-
-
-def broadcast(value, axis, source):
-    kept = jnp.where(lax.axis_index(axis) == source, value, 0).astype(value.dtype)
-    return lax.psum(kept, axis)
 
 
 def swap(value, row_count, distance):
@@ -177,13 +172,13 @@
     depth = reflectors.shape[1]
     capacity = (5 * block_count + 4 * row_count - 1) // (4 * row_count)
     slot_total = row_count * capacity
-    early = 7 * capacity // 10
+    early = 3 * capacity // 5
     share = 2 * depth // col_count
     half = row_count // 2
     order = list(range(half // 2, half)) + list(range(half, row_count)) + list(range(1, half // 2))
     early_parts = [(0, max(1, early // 6))]
     early_parts += [(early_parts[0][1], early - early_parts[0][1])]
-    late_parts = [(early + at, count) for at, count in pieces(capacity - early, 4)]
+    late_parts = [(early + at, count) for at, count in pieces(capacity - early, max(1, (capacity - early) // 2))]
 
     owner_of = band_owner[:, 0]
     position = jnp.arange(block_count, dtype=jnp.int32)
@@ -205,7 +200,8 @@
         packed = gather_blocks(z, *tables(at, count), len(order), count)
         raw[at] = [swap(item, row_count, d) for d, item in zip(order, packed)]
 
-    panels = [broadcast(reflectors, "col", owners[which]) for which in range(2)]
+    candidates = lax.all_gather(reflectors, "col", axis=0)
+    panels = [lax.dynamic_index_in_dim(candidates, owners[which], 0, keepdims=False) for which in range(2)]
     mine = jnp.concatenate([jnp.where(col == owners[which], t_factors, 0.0) for which in range(2)], axis=0)
     triangles = lax.psum(mine, "col")
 
@@ -216,10 +212,11 @@
         ],
         axis=0,
     )
-    products = lax.psum(partial_value.astype(jnp.bfloat16), "row").astype(jnp.float32)
-    gram = lax.psum(
-        lax.dot_general(panels[1], panels[0], contract_rows, preferred_element_type=jnp.float32), "row"
-    )
+    gram = lax.dot_general(panels[1], panels[0], contract_rows, preferred_element_type=jnp.float32)
+    gram = jnp.concatenate([jnp.zeros_like(gram), gram], axis=0)
+    partial_value = jnp.concatenate([partial_value.astype(jnp.bfloat16), gram.astype(jnp.bfloat16)], axis=1)
+    totals = lax.psum(partial_value, "row").astype(jnp.float32)
+    products, gram = totals[:, :width], totals[depth:, width:]
     first = jnp.dot(triangles[:depth], products[:depth], precision=lax.Precision.HIGHEST).astype(jnp.bfloat16)
     rest = products[depth:] - jnp.dot(gram, first.astype(jnp.float32), precision=lax.Precision.HIGHEST)
     second = jnp.dot(triangles[depth:], rest, precision=lax.Precision.HIGHEST).astype(jnp.bfloat16)

time: 1670 us -> 1520 us (0.910)
  the two profiles are of different devices: /device:TPU:0 before, /device:TPU:18 now
where the time goes in v2:
time: 1520 us
  waiting for transfers between devices  1180 us (78%)
  Pallas kernels  156 us (10%)
  starting transfers between devices  59.1 us (4%)
  local copies, waits for them, and re-layouts  48.3 us (3%)
  matrix products  42.6 us (3%)
  between operations  18.9 us (1%)
    ppermute x35, waiting for transfers between devices, swap(): lax.ppermute(value, 'row', [(s, s ^ distance) for s in range(row_count)])  890 us
    all_gather x1, waiting for transfers between devices, body(): candidates = lax.all_gather(reflectors, 'col', axis=0)  192 us
    psum x1, waiting for transfers between devices, body(): totals = lax.psum(partial_value, 'row').astype(jnp.float32)  102 us
    pallas_call x2, Pallas kernels, settle_there(): pl.pallas_call(functools.partial(settle_kernel, groups, count), grid_spec...  71.3 us
    pallas_call x3, Pallas kernels, finish_here(): pl.pallas_call(functools.partial(finish_kernel, groups, count), grid_spec...  59.9 us
    ppermute x35, starting transfers between devices, swap(): lax.ppermute(value, 'row', [(s, s ^ distance) for s in range(row_count)])  58.8 us
    dot_general x2, matrix products, body(): lax.dot_general(panel, eigvecs, contract_rows, preferred_element_type=jnp...  35.2 us
  transfers between devices with their start and end apart: 39, of which 18 were waited for; matrix products, arithmetic and copies ran while one was open for 6% of the time, Pallas kernels for 10%

profile of v2, /device:TPU:18, one launch (start us, length us, event | category | flops | bytes accessed | tf_op | source)
XLA Modules:
  0.0 1520.7 jit_solution(10515312211197795668)
XLA Ops:
  18.2 192.4 %all-gather.5.cloned.1.call-done = bf16[65536,256]{1,0:T(8,128)(2,1)} async-done(((bf16[16384,256]{1,0:T(8,128)(2,1)}), bf16[65536,256]{1,0:T(8,128)(2,1)}) %all-gather.5.cloned.1.call-update) | async-done | bytes 33554448 | tf_op jit(solution)/shard_map/all_gather | solution.py:203
  225.3 17.7 %convolution_convert_fusion.2 = bf16[256,1024]{1,0:T(8,128)(2,1)S(1)} fusion(bf16[16384,1024]{1,0:T(8,128)(2,1)} %param.5, bf16[1,16384,256]{2,1,0:T(8,128)(2,1)} %copy-done), kind=kOutput, calls=%fused_computation.9 | convolution fusion | flops 8590196736 | bytes 42467328 | tf_op jit(solution)/shard_map/dot_general | solution.py:210
  243.0 17.5 %convolution_convert_fusion.3 = bf16[256,1024]{1,0:T(8,128)(2,1)S(1)} fusion(bf16[16384,1024]{1,0:T(8,128)(2,1)} %param.5, bf16[1,16384,256]{2,1,0:T(8,128)(2,1)} %copy-done.1), kind=kOutput, calls=%fused_computation.10 | convolution fusion | flops 8590196736 | bytes 42467328 | tf_op jit(solution)/shard_map/dot_general | solution.py:210
  278.3 101.5 %all-reduce.6.cloned.1.call-done = bf16[512,1280]{1,0:T(8,128)(2,1)} async-done(((bf16[512,1280]{1,0:T(8,128)(2,1)}), bf16[512,1280]{1,0:T(8,128)(2,1)}) %all-reduce.6.cloned.1.call-update) | async-done | bytes 1310736 | tf_op jit(solution)/shard_map/psum | solution.py:218
  388.7 21.5 %shard_map.58 = (bf16[4,128,1024]{2,1,0:T(8,128)(2,1)}, bf16[4,128,1024]{2,1,0:T(8,128)(2,1)}, bf16[4,128,1024]{2,1,0:T(8,128)(2,1)}, bf16[4,128,1024]{2,1,0:T(8...) custom-call(s32[28]{0:T(128)} %get-tuple-element.132.block_ref, ...), custom_call_target="tpu_custom_call" | custom-call | tf_op jit(solution)/shard_map/pallas_call | solution.py:107
  419.5 15.7 %shard_map.60 = (bf16[10,128,1024]{2,1,0:T(8,128)(2,1)}, bf16[10,128,1024]{2,1,0:T(8,128)(2,1)}, bf16[10,128,1024]{2,1,0:T(8,128)(2,1)}, bf16[10,128,1024]{2,1,0...) custom-call(s32[70]{0:T(128)} %get-tuple-element.130.block_ref, ...), custom_call_target="tpu_custom_call" | custom-call | tf_op jit(solution)/shard_map/pallas_call | solution.py:69
  448.5 124.8 %collective-permute-done.refs_0_ = bf16[2,128,1024]{2,1,0:T(8,128)(2,1)S(1)} collective-permute-done((bf16[2,128,1024]{2,1,0:T(8,128)(2,1)}, bf16[2,128,1024]{2,1,0:T(8,128)(2,1)S(1)}, u32[]{:S(2)}, u32[]{:S(2)}) %collective-permute-start) | collective-permute-done | bytes 524320 | tf_op jit(solution)/shard_map/ppermute | solution.py:16
  588.8 38.4 %collective-permute-done.3.refs_3_ = bf16[2,128,1024]{2,1,0:T(8,128)(2,1)S(1)} collective-permute-done((bf16[2,128,1024]{2,1,0:T(8,128)(2,1)}, bf16[2,128,1024]{2,1,0:T(8,128)(2,1)S(1)}, u32[]{:S(2)}, u32[]{:S(2)}) %collective-permute-start.3) | collective-permute-done | bytes 524320 | tf_op jit(solution)/shard_map/ppermute | solution.py:16
  628.8 11.9 collective-permute-done.4.refs_4_
  640.7 66.3 %collective-permute-done.5.refs_5_ = bf16[2,128,1024]{2,1,0:T(8,128)(2,1)S(1)} collective-permute-done((bf16[2,128,1024]{2,1,0:T(8,128)(2,1)}, bf16[2,128,1024]{2,1,0:T(8,128)(2,1)S(1)}, u32[]{:S(2)}, u32[]{:S(2)}) %collective-permute-start.5) | collective-permute-done | bytes 524320 | tf_op jit(solution)/shard_map/ppermute | solution.py:16
  712.1 23.1 %shard_map.62 = (bf16[4,128,1024]{2,1,0:T(8,128)(2,1)}, bf16[4,128,1024]{2,1,0:T(8,128)(2,1)}, bf16[4,128,1024]{2,1,0:T(8,128)(2,1)}, bf16[4,128,1024]{2,1,0:T(8...) custom-call(s32[28]{0:T(128)} %get-tuple-element.128.block_ref, ...), custom_call_target="tpu_custom_call" | custom-call | tf_op jit(solution)/shard_map/pallas_call | solution.py:107
  735.2 195.4 %collective-permute-done.16.refs_2_ = bf16[10,128,1024]{2,1,0:T(8,128)(2,1)} collective-permute-done((bf16[10,128,1024]{2,1,0:T(8,128)(2,1)}, bf16[10,128,1024]{2,1,0:T(8,128)(2,1)}, u32[]{:S(2)}, u32[]{:S(2)}) %collective-permute-start.16) | collective-permute-done | bytes 2621472 | tf_op jit(solution)/shard_map/ppermute | solution.py:16
  934.4 52.4 %collective-permute-done.17.refs_3_ = bf16[10,128,1024]{2,1,0:T(8,128)(2,1)} collective-permute-done((bf16[10,128,1024]{2,1,0:T(8,128)(2,1)}, bf16[10,128,1024]{2,1,0:T(8,128)(2,1)}, u32[]{:S(2)}, u32[]{:S(2)}) %collective-permute-start.17) | collective-permute-done | bytes 2621472 | tf_op jit(solution)/shard_map/ppermute | solution.py:16
  991.5 53.8 %collective-permute-done.18.refs_4_ = bf16[10,128,1024]{2,1,0:T(8,128)(2,1)} collective-permute-done((bf16[10,128,1024]{2,1,0:T(8,128)(2,1)}, bf16[10,128,1024]{2,1,0:T(8,128)(2,1)}, u32[]{:S(2)}, u32[]{:S(2)}) %collective-permute-start.18) | collective-permute-done | bytes 2621472 | tf_op jit(solution)/shard_map/ppermute | solution.py:16
  1045.4 77.5 %collective-permute-done.19.refs_5_ = bf16[10,128,1024]{2,1,0:T(8,128)(2,1)} collective-permute-done((bf16[10,128,1024]{2,1,0:T(8,128)(2,1)}, bf16[10,128,1024]{2,1,0:T(8,128)(2,1)}, u32[]{:S(2)}, u32[]{:S(2)}) %collective-permute-start.19) | collective-permute-done | bytes 2621472 | tf_op jit(solution)/shard_map/ppermute | solution.py:16
  1127.2 84.3 %collective-permute-done.23 = bf16[4,128,1024]{2,1,0:T(8,128)(2,1)S(1)} collective-permute-done((bf16[4,128,1024]{2,1,0:T(8,128)(2,1)}, bf16[4,128,1024]{2,1,0:T(8,128)(2,1)S(1)}, u32[]{:S(2)}, u32[]{:S(2)}) %collective-permute-start.23) | collective-permute-done | bytes 1048608 | tf_op jit(solution)/shard_map/ppermute | solution.py:16
  1215.3 18.8 %collective-permute-done.24 = bf16[4,128,1024]{2,1,0:T(8,128)(2,1)S(1)} collective-permute-done((bf16[4,128,1024]{2,1,0:T(8,128)(2,1)}, bf16[4,128,1024]{2,1,0:T(8,128)(2,1)S(1)}, u32[]{:S(2)}, u32[]{:S(2)}) %collective-permute-start.24) | collective-permute-done | bytes 1048608 | tf_op jit(solution)/shard_map/ppermute | solution.py:16
  1240.6 15.4 %shard_map.55.owned_ref = bf16[160,128,1024]{2,1,0:T(8,128)(2,1)} custom-call(s32[20]{0:T(128)} %get-tuple-element.138.block_ref, s32[20]{0:T(128)} %get-tuple-element.137.filled_ref, s32[1]{0:T(128)} %bitcast.5.base_ref, bf16[128,128,1024]{2,1,0:T(8,128)(2,1)} %bitcast.56, bf16[128,128,256]{2,1,0:T(8,128)(2,1)} %bitcast.64, ...), custom_call_target="tpu_custom_call" | custom-call | tf_op jit(solution)/shard_map/pallas_call | solution.py:107
  1256.0 13.7 shard_map.59.owned_ref
  1269.6 57.6 %shard_map.61 = bf16[160,128,1024]{2,1,0:T(8,128)(2,1)} custom-call(s32[70]{0:T(128)} %concatenate.43.slot_ref, bf16[160,128,1024]{2,1,0:T(8,128)(2,1)} %shard_map.59.owned_ref, bf16[10,128,1024]{2,1,0:T(8,128)(2,1)} %copy-done.3, bf16[10,128,1024]{2,1,0:T(8,128)(2,1)} %collective-permute-done.15.refs_1_, ...), custom_call_target="tpu_custom_call", output_to_operand_aliasing={{}: (1, {})} | custom-call | tf_op jit(solution)/shard_map/pallas_call | solution.py:146
  1351.2 92.2 %collective-permute-done.30 = bf16[4,128,1024]{2,1,0:T(8,128)(2,1)S(1)} collective-permute-done((bf16[4,128,1024]{2,1,0:T(8,128)(2,1)}, bf16[4,128,1024]{2,1,0:T(8,128)(2,1)S(1)}, u32[]{:S(2)}, u32[]{:S(2)}) %collective-permute-start.30) | collective-permute-done | bytes 1048608 | tf_op jit(solution)/shard_map/ppermute | solution.py:16
  1444.5 21.4 %collective-permute-done.31 = bf16[4,128,1024]{2,1,0:T(8,128)(2,1)S(1)} collective-permute-done((bf16[4,128,1024]{2,1,0:T(8,128)(2,1)}, bf16[4,128,1024]{2,1,0:T(8,128)(2,1)S(1)}, u32[]{:S(2)}, u32[]{:S(2)}) %collective-permute-start.31) | collective-permute-done | bytes 1048608 | tf_op jit(solution)/shard_map/ppermute | solution.py:16
  1466.9 22.9 %collective-permute-done.32 = bf16[4,128,1024]{2,1,0:T(8,128)(2,1)S(1)} collective-permute-done((bf16[4,128,1024]{2,1,0:T(8,128)(2,1)}, bf16[4,128,1024]{2,1,0:T(8,128)(2,1)S(1)}, u32[]{:S(2)}, u32[]{:S(2)}) %collective-permute-start.32) | collective-permute-done | bytes 1048608 | tf_op jit(solution)/shard_map/ppermute | solution.py:16
  1490.9 21.2 %collective-permute-done.33 = bf16[4,128,1024]{2,1,0:T(8,128)(2,1)S(1)} collective-permute-done((bf16[4,128,1024]{2,1,0:T(8,128)(2,1)S(1)}, bf16[4,128,1024]{2,1,0:T(8,128)(2,1)S(1)}, u32[]{:S(2)}, u32[]{:S(2)}) %collective-permute-start.33) | collective-permute-done | bytes 1048608 | tf_op jit(solution)/shard_map/ppermute | solution.py:16
  (191 shorter events, 144.5 us)
Async XLA Ops:
  6.5 204.0 %all-gather.5.cloned.1.call-start = ((), (), s32[]{:S(2)}) async-start(), calls=%async_computation.2 | async-start | bytes 41943040 | tf_op jit(solution)/shard_map/all_gather | solution.py:203
  7.3 271.1 %all-reduce.4.cloned.1.call-start = ((), (), s32[]{:S(2)}) async-start(), calls=%async_computation | async-start | bytes 1048576 | tf_op jit(solution)/shard_map/psum | solution.py:206
  10.1 369.7 %all-reduce.6.cloned.1.call-start = ((), (), s32[]{:S(2)}) async-start(), calls=%async_computation.1 | async-start | bytes 2621440 | tf_op jit(solution)/shard_map/psum | solution.py:218
  261.6 994.3 %all-gather.7.cloned.1.call-start = ((), (), s32[]{:S(2)}) async-start(), calls=%async_computation.3 | async-start | bytes 13762560 | tf_op jit(solution)/shard_map/all_gather | solution.py:239
  274.8 135.4 %collective-permute-start.9 = (bf16[12,128,128]{2,1,0:T(8,128)(2,1)}, bf16[12,128,128]{2,1,0:T(8,128)(2,1)S(1)}, u32[]{:S(2)}, u32[]{:S(2)}) collective-permute-start(bf16[12,128,128]{2,1,0:T(8,128)(2,1)} %get-tuple-element.56), channel_id=1, source_target_pairs={{0,16},{4,20},{8,24},{12,28},{16,0},{20,4},{24,8},{28,12},{1,17},{... | collective-permute-start | bytes 1179656 | tf_op jit(solution)/shard_map/ppermute | solution.py:16
  275.3 134.9 %collective-permute-start.10 = (bf16[12,128,128]{2,1,0:T(8,128)(2,1)}, bf16[12,128,128]{2,1,0:T(8,128)(2,1)S(1)}, u32[]{:S(2)}, u32[]{:S(2)}) collective-permute-start(bf16[12,128,128]{2,1,0:T(8,128)(2,1)} %get-tuple-element.57), channel_id=1, source_target_pairs={{0,20},{4,16},{8,28},{12,24},{16,4},{20,0},{24,12},{28,8},{1,21},{... | collective-permute-start | bytes 1179656 | tf_op jit(solution)/shard_map/ppermute | solution.py:16
  435.2 274.3 %collective-permute-start.14 = (bf16[10,128,1024]{2,1,0:T(8,128)(2,1)}, bf16[10,128,1024]{2,1,0:T(8,128)(2,1)S(1)}, u32[]{:S(2)}, u32[]{:S(2)}) collective-permute-start(bf16[10,128,1024]{2,1,0:T(8,128)(2,1)} %get-tuple-element.75), channel_id=1, source_target_pairs={{0,8},{4,12},{8,0},{12,4},{16,24},{20,28},{24,16},{28,20},{1,9},{5... | collective-permute-start | bytes 7864328 | tf_op jit(solution)/shard_map/ppermute | solution.py:16
  437.1 274.1 %collective-permute-start.15 = (bf16[10,128,1024]{2,1,0:T(8,128)(2,1)}, bf16[10,128,1024]{2,1,0:T(8,128)(2,1)}, u32[]{:S(2)}, u32[]{:S(2)}) collective-permute-start(bf16[10,128,1024]{2,1,0:T(8,128)(2,1)} %get-tuple-element.76), channel_id=1, source_target_pairs={{0,12},{4,8},{8,4},{12,0},{16,28},{20,24},{24,20},{28,16},{1,13},{... | collective-permute-start | bytes 7864328 | tf_op jit(solution)/shard_map/ppermute | solution.py:16
  445.1 137.7 %collective-permute-start.1 = (bf16[2,128,1024]{2,1,0:T(8,128)(2,1)}, bf16[2,128,1024]{2,1,0:T(8,128)(2,1)S(1)}, u32[]{:S(2)}, u32[]{:S(2)}) collective-permute-start(bf16[2,128,1024]{2,1,0:T(8,128)(2,1)} %get-tuple-element.48), channel_id=1, source_target_pairs={{0,12},{4,8},{8,4},{12,0},{16,28},{20,24},{24,20},{28,16},{1,13},{... | collective-permute-start | bytes 1572872 | tf_op jit(solution)/shard_map/ppermute | solution.py:16
  445.7 140.6 %collective-permute-start.2 = (bf16[2,128,1024]{2,1,0:T(8,128)(2,1)}, bf16[2,128,1024]{2,1,0:T(8,128)(2,1)S(1)}, u32[]{:S(2)}, u32[]{:S(2)}) collective-permute-start(bf16[2,128,1024]{2,1,0:T(8,128)(2,1)} %get-tuple-element.49), channel_id=1, source_target_pairs={{0,16},{4,20},{8,24},{12,28},{16,0},{20,4},{24,8},{28,12},{1,17},{... | collective-permute-start | bytes 1572872 | tf_op jit(solution)/shard_map/ppermute | solution.py:16
  640.7 289.9 %collective-permute-start.16 = (bf16[10,128,1024]{2,1,0:T(8,128)(2,1)}, bf16[10,128,1024]{2,1,0:T(8,128)(2,1)}, u32[]{:S(2)}, u32[]{:S(2)}) collective-permute-start(bf16[10,128,1024]{2,1,0:T(8,128)(2,1)} %get-tuple-element.77), channel_id=1, source_target_pairs={{0,16},{4,20},{8,24},{12,28},{16,0},{20,4},{24,8},{28,12},{1,17},{... | collective-permute-start | bytes 7864328 | tf_op jit(solution)/shard_map/ppermute | solution.py:16
  707.0 279.8 %collective-permute-start.17 = (bf16[10,128,1024]{2,1,0:T(8,128)(2,1)}, bf16[10,128,1024]{2,1,0:T(8,128)(2,1)}, u32[]{:S(2)}, u32[]{:S(2)}) collective-permute-start(bf16[10,128,1024]{2,1,0:T(8,128)(2,1)} %get-tuple-element.78), channel_id=1, source_target_pairs={{0,20},{4,16},{8,28},{12,24},{16,4},{20,0},{24,12},{28,8},{1,21},{... | collective-permute-start | bytes 7864328 | tf_op jit(solution)/shard_map/ppermute | solution.py:16
  707.0 338.3 %collective-permute-start.18 = (bf16[10,128,1024]{2,1,0:T(8,128)(2,1)}, bf16[10,128,1024]{2,1,0:T(8,128)(2,1)}, u32[]{:S(2)}, u32[]{:S(2)}) collective-permute-start(bf16[10,128,1024]{2,1,0:T(8,128)(2,1)} %get-tuple-element.79), channel_id=1, source_target_pairs={{0,24},{4,28},{8,16},{12,20},{16,8},{20,12},{24,0},{28,4},{1,25},{... | collective-permute-start | bytes 7864328 | tf_op jit(solution)/shard_map/ppermute | solution.py:16
  709.4 413.4 %collective-permute-start.19 = (bf16[10,128,1024]{2,1,0:T(8,128)(2,1)}, bf16[10,128,1024]{2,1,0:T(8,128)(2,1)}, u32[]{:S(2)}, u32[]{:S(2)}) collective-permute-start(bf16[10,128,1024]{2,1,0:T(8,128)(2,1)} %get-tuple-element.80), channel_id=1, source_target_pairs={{0,28},{4,24},{8,20},{12,16},{16,12},{20,8},{24,4},{28,0},{1,29},{... | collective-permute-start | bytes 7864328 | tf_op jit(solution)/shard_map/ppermute | solution.py:16
  711.3 411.6 %collective-permute-start.20 = (bf16[10,128,1024]{2,1,0:T(8,128)(2,1)}, bf16[10,128,1024]{2,1,0:T(8,128)(2,1)}, u32[]{:S(2)}, u32[]{:S(2)}) collective-permute-start(bf16[10,128,1024]{2,1,0:T(8,128)(2,1)} %get-tuple-element.81), channel_id=1, source_target_pairs={{0,4},{4,0},{8,12},{12,8},{16,20},{20,16},{24,28},{28,24},{1,5},{5... | collective-permute-start | bytes 7864328 | tf_op jit(solution)/shard_map/ppermute | solution.py:16
  930.6 194.7 %collective-permute-start.21 = (bf16[4,128,1024]{2,1,0:T(8,128)(2,1)}, bf16[4,128,1024]{2,1,0:T(8,128)(2,1)S(1)}, u32[]{:S(2)}, u32[]{:S(2)}) collective-permute-start(bf16[4,128,1024]{2,1,0:T(8,128)(2,1)} %get-tuple-element.82), channel_id=1, source_target_pairs={{0,8},{4,12},{8,0},{12,4},{16,24},{20,28},{24,16},{28,20},{1,9},{5... | collective-permute-start | bytes 3145736 | tf_op jit(solution)/shard_map/ppermute | solution.py:16
  986.8 140.3 %collective-permute-start.22 = (bf16[4,128,1024]{2,1,0:T(8,128)(2,1)}, bf16[4,128,1024]{2,1,0:T(8,128)(2,1)S(1)}, u32[]{:S(2)}, u32[]{:S(2)}) collective-permute-start(bf16[4,128,1024]{2,1,0:T(8,128)(2,1)} %get-tuple-element.83), channel_id=1, source_target_pairs={{0,12},{4,8},{8,4},{12,0},{16,28},{20,24},{24,20},{28,16},{1,13},{... | collective-permute-start | bytes 3145736 | tf_op jit(solution)/shard_map/ppermute | solution.py:16
  1045.4 166.2 %collective-permute-start.23 = (bf16[4,128,1024]{2,1,0:T(8,128)(2,1)}, bf16[4,128,1024]{2,1,0:T(8,128)(2,1)S(1)}, u32[]{:S(2)}, u32[]{:S(2)}) collective-permute-start(bf16[4,128,1024]{2,1,0:T(8,128)(2,1)} %get-tuple-element.84), channel_id=1, source_target_pairs={{0,16},{4,20},{8,24},{12,28},{16,0},{20,4},{24,8},{28,12},{1,17},{... | collective-permute-start | bytes 3145736 | tf_op jit(solution)/shard_map/ppermute | solution.py:16
  1122.9 206.8 %collective-permute-start.25 = (bf16[4,128,1024]{2,1,0:T(8,128)(2,1)}, bf16[4,128,1024]{2,1,0:T(8,128)(2,1)S(1)}, u32[]{:S(2)}, u32[]{:S(2)}) collective-permute-start(bf16[4,128,1024]{2,1,0:T(8,128)(2,1)} %get-tuple-element.86), channel_id=1, source_target_pairs={{0,24},{4,28},{8,16},{12,20},{16,8},{20,12},{24,0},{28,4},{1,25},{... | collective-permute-start | bytes 3145736 | tf_op jit(solution)/shard_map/ppermute | solution.py:16
  1125.3 206.6 %collective-permute-start.26 = (bf16[4,128,1024]{2,1,0:T(8,128)(2,1)}, bf16[4,128,1024]{2,1,0:T(8,128)(2,1)}, u32[]{:S(2)}, u32[]{:S(2)}) collective-permute-start(bf16[4,128,1024]{2,1,0:T(8,128)(2,1)} %get-tuple-element.87), channel_id=1, source_target_pairs={{0,28},{4,24},{8,20},{12,16},{16,12},{20,8},{24,4},{28,0},{1,29},{... | collective-permute-start | bytes 3145736 | tf_op jit(solution)/shard_map/ppermute | solution.py:16
  1127.1 208.9 %collective-permute-start.27 = (bf16[4,128,1024]{2,1,0:T(8,128)(2,1)}, bf16[4,128,1024]{2,1,0:T(8,128)(2,1)}, u32[]{:S(2)}, u32[]{:S(2)}) collective-permute-start(bf16[4,128,1024]{2,1,0:T(8,128)(2,1)} %get-tuple-element.88), channel_id=1, source_target_pairs={{0,4},{4,0},{8,12},{12,8},{16,20},{20,16},{24,28},{28,24},{1,5},{5... | collective-permute-start | bytes 3145736 | tf_op jit(solution)/shard_map/ppermute | solution.py:16
  1336.1 153.8 %collective-permute-start.32 = (bf16[4,128,1024]{2,1,0:T(8,128)(2,1)}, bf16[4,128,1024]{2,1,0:T(8,128)(2,1)S(1)}, u32[]{:S(2)}, u32[]{:S(2)}) collective-permute-start(bf16[4,128,1024]{2,1,0:T(8,128)(2,1)} %get-tuple-element.65), channel_id=1, source_target_pairs={{0,24},{4,28},{8,16},{12,20},{16,8},{20,12},{24,0},{28,4},{1,25},{... | collective-permute-start | bytes 3145736 | tf_op jit(solution)/shard_map/ppermute | solution.py:16
  1339.6 172.4 %collective-permute-start.33 = (bf16[4,128,1024]{2,1,0:T(8,128)(2,1)S(1)}, bf16[4,128,1024]{2,1,0:T(8,128)(2,1)S(1)}, u32[]{:S(2)}, u32[]{:S(2)}) collective-permute-start(bf16[4,128,1024]{2,1,0:T(8,128)(2,1)S(1)} %copy-done.24), channel_id=1, source_target_pairs={{0,28},{4,24},{8,20},{12,16},{16,12},{20,8},{24,4},{28,0},{1,29},{... | collective-permute-start | bytes 3145736 | tf_op jit(solution)/shard_map/ppermute | solution.py:16
  1340.9 172.2 %collective-permute-start.34 = (bf16[4,128,1024]{2,1,0:T(8,128)(2,1)S(1)}, bf16[4,128,1024]{2,1,0:T(8,128)(2,1)S(1)}, u32[]{:S(2)}, u32[]{:S(2)}) collective-permute-start(bf16[4,128,1024]{2,1,0:T(8,128)(2,1)S(1)} %copy-done.23), channel_id=1, source_target_pairs={{0,4},{4,0},{8,12},{12,8},{16,20},{20,16},{24,28},{28,24},{1,5},{5... | collective-permute-start | bytes 3145736 | tf_op jit(solution)/shard_map/ppermute | solution.py:16
  (41 other events, 3104.3 us)
Sparse Core Ops, SparseCore 0:
  8.9 201.6 all-gather.4
  212.9 33.5 all-reduce.3
  261.8 118.0 all-reduce.5
  418.5 73.4 all-gather.6

commit v3 on v2

--- a/solution.py
+++ b/solution.py
@@ -14,10 +14,6 @@
 
 def swap(value, row_count, distance):
     return lax.ppermute(value, "row", [(s, s ^ distance) for s in range(row_count)])
-
-
-def pieces(total, size):
-    return [(at, min(size, total - at)) for at in range(0, total, size)]
 
 
 def gather_kernel(groups, count, block_ref, filled_ref, source, *rest):
@@ -164,6 +160,114 @@
     )(slots, owned, *z_list, v, y)
 
 
+def relay_kernel(groups, lanes, per_lane, index_ref, filled_ref, *rest):
+    sources, rest = rest[:lanes], rest[lanes:]
+    outs, (stage, in_sems, out_sems) = rest[:groups], rest[groups:]
+    count = lanes * per_lane
+
+    def inward(k):
+        return pltpu.make_async_copy(sources[k % count // per_lane].at[index_ref[k]], stage.at[k], in_sems.at[k])
+
+    def outward(k):
+        return pltpu.make_async_copy(stage.at[k], outs[k // count].at[k % count], out_sems.at[k])
+
+    for k in range(groups * count):
+
+        @pl.when(filled_ref[k] > 0)
+        def _():
+            inward(k).start()
+
+    for k in range(groups * count):
+
+        @pl.when(filled_ref[k] > 0)
+        def _():
+            inward(k).wait()
+
+        @pl.when(filled_ref[k] <= 0)
+        def _():
+            stage[k] = jnp.zeros(stage.shape[1:], stage.dtype)
+
+        outward(k).start()
+    for k in range(groups * count):
+        outward(k).wait()
+
+
+def relay_blocks(sources, index, filled, groups, per_lane):
+    any_spec = pl.BlockSpec(memory_space=pl.ANY)
+    smem_spec = pl.BlockSpec(memory_space=pltpu.SMEM)
+    lanes, block, dtype = len(sources), sources[0].shape[1:], sources[0].dtype
+    total = groups * lanes * per_lane
+    return pl.pallas_call(
+        functools.partial(relay_kernel, groups, lanes, per_lane),
+        out_shape=[jax.ShapeDtypeStruct((lanes * per_lane,) + block, dtype)] * groups,
+        in_specs=[smem_spec, smem_spec] + [any_spec] * lanes,
+        out_specs=[any_spec] * groups,
+        scratch_shapes=[
+            pltpu.VMEM((total,) + block, dtype),
+            pltpu.SemaphoreType.DMA((total,)),
+            pltpu.SemaphoreType.DMA((total,)),
+        ],
+        compiler_params=pltpu.CompilerParams(vmem_limit_bytes=56 * 2**20),
+    )(index, filled, *sources)
+
+
+def fill_kernel(origins, choice_ref, slot_ref, owned_ref, *rest):
+    arrays = len(rest) - 4
+    sources, (out_ref, stage, in_sems, out_sems) = rest[:arrays], rest[arrays:]
+    total = stage.shape[0]
+    for k in range(total):
+        for option, (array, item) in enumerate(origins[k]):
+
+            @pl.when(choice_ref[k] == option + 1)
+            def _():
+                pltpu.make_async_copy(sources[array].at[item], stage.at[k], in_sems.at[k]).start()
+
+    for k in range(total):
+
+        @pl.when(choice_ref[k] > 0)
+        def _():
+            pltpu.make_async_copy(sources[0].at[0], stage.at[k], in_sems.at[k]).wait()
+
+        @pl.when(choice_ref[k] <= 0)
+        def _():
+            stage[k] = jnp.zeros(stage.shape[1:], stage.dtype)
+
+        pltpu.make_async_copy(stage.at[k], out_ref.at[slot_ref[k]], out_sems.at[k]).start()
+    for k in range(total):
+        pltpu.make_async_copy(stage.at[k], out_ref.at[slot_ref[k]], out_sems.at[k]).wait()
+
+
+def fill_slots(owned, sources, origins, choice, slots):
+    any_spec = pl.BlockSpec(memory_space=pl.ANY)
+    smem_spec = pl.BlockSpec(memory_space=pltpu.SMEM)
+    total = len(origins)
+    return pl.pallas_call(
+        functools.partial(fill_kernel, origins),
+        out_shape=jax.ShapeDtypeStruct(owned.shape, owned.dtype),
+        in_specs=[smem_spec, smem_spec, any_spec] + [any_spec] * len(sources),
+        out_specs=any_spec,
+        scratch_shapes=[
+            pltpu.VMEM((total,) + owned.shape[1:], owned.dtype),
+            pltpu.SemaphoreType.DMA((total,)),
+            pltpu.SemaphoreType.DMA((total,)),
+        ],
+        input_output_aliases={2: 0},
+    )(choice, slots, owned, *sources)
+
+
+def match_spares(counts, low, base, top):
+    streams = counts.shape[0]
+    spare = ((low + jnp.arange(base - low))[None, :] >= counts[:, None]).reshape(-1).astype(jnp.int32)
+    over = ((base + jnp.arange(top - base))[None, :] < counts[:, None]).reshape(-1).astype(jnp.int32)
+
+    def rank(flags):
+        k = jnp.arange(flags.shape[0])
+        return jnp.sum(flags[None, :] * (k[None, :] < k[:, None]), axis=1)
+
+    hit = spare[:, None] * over[None, :] * (rank(spare)[:, None] == rank(over)[None, :])
+    return hit.reshape(streams, base - low, streams, top - base), jnp.sum(over) <= jnp.sum(spare)
+
+
 def body(eigvecs, reflectors, t_factors, owners, band_owner):
     row_count, col_count = lax.axis_size("row"), lax.axis_size("col")
     me, col = lax.axis_index("row"), lax.axis_index("col")
@@ -172,13 +276,15 @@
     depth = reflectors.shape[1]
     capacity = (5 * block_count + 4 * row_count - 1) // (4 * row_count)
     slot_total = row_count * capacity
-    early = 3 * capacity // 5
+    early = 9 * capacity // 20
+    base = capacity - capacity // 10
+    low = early + max(1, 3 * (capacity - early) // 11)
     share = 2 * depth // col_count
     half = row_count // 2
-    order = list(range(half // 2, half)) + list(range(half, row_count)) + list(range(1, half // 2))
+    near, far = list(range(1, half)), list(range(half, row_count))
+    order = near[half // 2 - 1 :] + far + near[: half // 2 - 1]
     early_parts = [(0, max(1, early // 6))]
     early_parts += [(early_parts[0][1], early - early_parts[0][1])]
-    late_parts = [(early + at, count) for at, count in pieces(capacity - early, max(1, (capacity - early) // 2))]
 
     owner_of = band_owner[:, 0]
     position = jnp.arange(block_count, dtype=jnp.int32)
@@ -188,8 +294,10 @@
     hits = (slot_index[None, :] == jnp.arange(slot_total, dtype=jnp.int32)[:, None]).astype(jnp.int32)
     slot_table = jnp.stack([jnp.sum(hits * position[None, :], axis=1), jnp.sum(hits, axis=1)])
 
-    def tables(at, count):
-        starts = [(me ^ d) * capacity + at for d in order]
+    counts = jnp.sum((owner_of[:, None] == jnp.arange(row_count)[None, :]).astype(jnp.int32), axis=0)
+
+    def tables(at, count, distances=None):
+        starts = [(me ^ d) * capacity + at for d in distances or order]
         both = jnp.concatenate([lax.dynamic_slice(slot_table, (0, s), (2, count)) for s in starts], axis=1)
         return both[0], both[1]
 
@@ -215,8 +323,11 @@
     gram = lax.dot_general(panels[1], panels[0], contract_rows, preferred_element_type=jnp.float32)
     gram = jnp.concatenate([jnp.zeros_like(gram), gram], axis=0)
     partial_value = jnp.concatenate([partial_value.astype(jnp.bfloat16), gram.astype(jnp.bfloat16)], axis=1)
-    totals = lax.psum(partial_value, "row").astype(jnp.float32)
-    products, gram = totals[:, :width], totals[depth:, width:]
+    told = jnp.where(jnp.arange(16 * ((row_count + 15) // 16))[:, None] == me, counts[None, :], 0)
+    told = jnp.pad(told.astype(jnp.bfloat16), ((0, 0), (0, width + depth - row_count)))
+    totals = lax.psum(jnp.concatenate([partial_value, told], axis=0), "row").astype(jnp.float32)
+    products, gram = totals[: 2 * depth, :width], totals[depth : 2 * depth, width:]
+    all_counts = totals[2 * depth : 2 * depth + row_count, :row_count].astype(jnp.int32)
     first = jnp.dot(triangles[:depth], products[:depth], precision=lax.Precision.HIGHEST).astype(jnp.bfloat16)
     rest = products[depth:] - jnp.dot(gram, first.astype(jnp.float32), precision=lax.Precision.HIGHEST)
     second = jnp.dot(triangles[depth:], rest, precision=lax.Precision.HIGHEST).astype(jnp.bfloat16)
@@ -230,10 +341,23 @@
     v0 = panels[0].reshape(block_count, ROWS, depth)
     v1 = panels[1].reshape(block_count, ROWS, depth)
 
+    overflow = capacity - base
+    cross = jnp.stack([lax.dynamic_index_in_dim(counts, me ^ d, 0, keepdims=False) for d in far])
+    first_block, first_filled = tables(low, base - low, far)
+    if overflow:
+        hit, _ = match_spares(cross, low, base, capacity)
+        hit = hit.reshape(-1, len(far) * overflow)
+        spill_block, _ = tables(base, overflow, far)
+        first_block = first_block + jnp.sum(hit * spill_block[None, :], axis=1)
+        first_filled = first_filled + jnp.sum(hit, axis=1)
+
     late = {}
-    for at, count in late_parts:
-        done = finish_here(z, v0, v1, update, *tables(at, count), len(order), count)
-        late[at] = [swap(item, row_count, d) for d, item in zip(order, done)]
+    done = finish_here(z, v0, v1, update, first_block, first_filled, len(far), base - low)
+    late["far"] = [swap(item, row_count, d) for d, item in zip(far, done)]
+    done = finish_here(z, v0, v1, update, *tables(low, capacity - low, near), len(near), capacity - low)
+    late["near"] = [swap(item, row_count, d) for d, item in zip(near, done)]
+    done = finish_here(z, v0, v1, update, *tables(early, low - early), len(order), low - early)
+    late["last"] = [swap(item, row_count, d) for d, item in zip(order, done)]
 
     slim_list, _ = lax.optimization_barrier((slim_list, done))
     wide_there = lax.all_gather(jnp.concatenate(slim_list, axis=0), "col", axis=0)
@@ -243,9 +367,62 @@
     for at, count in early_parts:
         slots = jnp.concatenate([(me ^ d) * capacity + at + jnp.arange(count, dtype=jnp.int32) for d in order])
         owned = settle_there(owned, raw[at], wide_there, update, at, early, slots)
-    for at, count in late_parts:
-        for d, item in zip(order, late[at]):
-            owned = lax.dynamic_update_slice(owned, item, ((me ^ d) * capacity + at, 0, 0))
+
+    def place(owned, distance, at, value):
+        return lax.dynamic_update_slice(owned, value, ((me ^ distance) * capacity + at, 0, 0))
+
+    if overflow:
+        pairs = (jnp.arange(row_count)[:, None] ^ jnp.asarray(far)[None, :])[:, :, None] == jnp.arange(row_count)
+        crossing = jnp.sum(all_counts[:, None, :] * pairs, axis=2)
+        hits, fits = jax.vmap(lambda c: match_spares(c, low, base, capacity))(crossing)
+        fits = jnp.all(fits)
+        seen = [lax.dynamic_index_in_dim(hits, me ^ d, 0, keepdims=False) for d in far]
+        index, filled = [], []
+        for d in near:
+            for stream in range(len(far)):
+                found = seen[stream][stream, :, (far[stream] ^ d) - half, :]
+                index.append(jnp.sum(found * jnp.arange(base - low)[:, None], axis=0))
+                filled.append(jnp.sum(found, axis=0))
+        relayed = relay_blocks(late["far"], jnp.concatenate(index), jnp.concatenate(filled), len(near), overflow)
+        relayed = [swap(item, row_count, d) for d, item in zip(near, relayed)]
+
+    for d, item in zip(near, late["near"]):
+        owned = place(owned, d, low, item)
+    for d, item in zip(far, late["far"]):
+        if overflow:
+            held = lax.dynamic_index_in_dim(all_counts[:, :], me ^ d, 0, keepdims=False)
+            held = lax.dynamic_index_in_dim(held, me, 0, keepdims=False)
+            item = jnp.where((low + jnp.arange(base - low) < held)[:, None, None], item, 0).astype(item.dtype)
+        owned = place(owned, d, low, item)
+
+    if overflow:
+        gate, owned = lax.optimization_barrier((fits, owned))
+
+        def direct():
+            sent = finish_here(z, v0, v1, update, *tables(base, overflow, far), len(far), overflow)
+            return [swap(item, row_count, d) for d, item in zip(far, sent)]
+
+        def nothing():
+            return [jnp.zeros((overflow, ROWS, width), z.dtype)] * len(far)
+
+        straight = lax.cond(gate, nothing, direct)
+    for d, item in zip(order, late["last"]):
+        owned = place(owned, d, early, item)
+
+    if overflow:
+        origins, choice, slots = [], [], []
+        for owner, d in enumerate(far):
+            for item in range(overflow):
+                options, picked = [], 0
+                for number, step in enumerate(near):
+                    stream = (d ^ step) - half
+                    options.append((number, stream * overflow + item))
+                    picked = picked + (number + 1) * jnp.sum(seen[owner][stream, :, owner, item])
+                options.append((len(near) + owner, item))
+                origins.append(tuple(options))
+                choice.append(jnp.where(fits, picked, len(options)))
+                slots.append((me ^ d) * capacity + base + item)
+        owned = fill_slots(owned, relayed + straight, tuple(origins), jnp.stack(choice), jnp.stack(slots))
     return owned.reshape(slot_total * ROWS, width)
 
 

time: 1520 us -> 1400 us (0.921)
  the two profiles are of different devices: /device:TPU:18 before, /device:TPU:0 now
where the time goes in v3:
time: 1400 us; the launch traced here: 1390 us
  waiting for transfers between devices  840 us (60%)
  starting transfers between devices  231 us (16%)
  Pallas kernels  151 us (11%)
  local copies, waits for them, and re-layouts  55.3 us (4%)
  matrix products  41.6 us (3%)
  between operations  40.3 us (3%)
  other arithmetic  33.2 us (2%)
    ppermute x38, waiting for transfers between devices, swap(): lax.ppermute(value, 'row', [(s, s ^ distance) for s in range(row_count)])  544 us
    ppermute x38, starting transfers between devices, swap(): lax.ppermute(value, 'row', [(s, s ^ distance) for s in range(row_count)])  231 us
    all_gather x1, waiting for transfers between devices, body(): candidates = lax.all_gather(reflectors, 'col', axis=0)  197 us
    psum x1, waiting for transfers between devices, body(): lax.psum(jnp.concatenate([partial_value, told], axis=0), 'row')  98.4 us
    pallas_call x4, Pallas kernels, finish_here(): pl.pallas_call(functools.partial(finish_kernel, groups, count), grid_spec...  70.5 us
    pallas_call x2, Pallas kernels, settle_there(): pl.pallas_call(functools.partial(settle_kernel, groups, count), grid_spec...  53.6 us
    dot_general x2, matrix products, body(): lax.dot_general(panel, eigvecs, contract_rows, preferred_element_type=jnp...  35.2 us
  transfers between devices with their start and end apart: 42, of which 13 were waited for; matrix products, arithmetic and copies ran while one was open for 8% of the time, Pallas kernels for 11%

profile of v3, /device:TPU:0, one launch (start us, length us, event | category | flops | bytes accessed | tf_op | source)
XLA Modules:
  0.0 1392.7 jit_solution(3760798699368567618)
XLA Ops:
  16.6 196.6 %all-gather.5.cloned.1.call-done = bf16[65536,256]{1,0:T(8,128)(2,1)} async-done(((bf16[16384,256]{1,0:T(8,128)(2,1)}), bf16[65536,256]{1,0:T(8,128)(2,1)}) %all-gather.5.cloned.1.call-update) | async-done | bytes 33554448 | tf_op jit(solution)/shard_map/all_gather | solution.py:311
  213.2 6.5 constant_dynamic-slice_fusion.89
  227.9 17.7 %convolution_convert_fusion.2 = bf16[256,1024]{1,0:T(8,128)(2,1)S(1)} fusion(bf16[16384,1024]{1,0:T(8,128)(2,1)} %param.8, bf16[1,16384,256]{2,1,0:T(8,128)(2,1)} %copy-done.1), kind=kOutput, calls=%fused_computation.26 | convolution fusion | flops 8590196736 | bytes 42467328 | tf_op jit(solution)/shard_map/dot_general | solution.py:318
  245.6 17.5 %convolution_convert_fusion.3 = bf16[256,1024]{1,0:T(8,128)(2,1)S(1)} fusion(bf16[16384,1024]{1,0:T(8,128)(2,1)} %param.8, bf16[1,16384,256]{2,1,0:T(8,128)(2,1)} %copy-done), kind=kOutput, calls=%fused_computation.27 | convolution fusion | flops 8590196736 | bytes 42467328 | tf_op jit(solution)/shard_map/dot_general | solution.py:318
  282.7 98.4 %all-reduce.5.cloned.1.call-done = bf16[528,1280]{1,0:T(8,128)(2,1)} async-done(((bf16[528,1280]{1,0:T(8,128)(2,1)}), bf16[528,1280]{1,0:T(8,128)(2,1)}) %all-reduce.5.cloned.1.call-update) | async-done | bytes 1351696 | tf_op jit(solution)/shard_map/psum | solution.py:328
  389.9 18.2 %shard_map.67 = (bf16[3,128,1024]{2,1,0:T(8,128)(2,1)}, bf16[3,128,1024]{2,1,0:T(8,128)(2,1)}, bf16[3,128,1024]{2,1,0:T(8,128)(2,1)}, bf16[3,128,1024]{2,1,0:T(8...) custom-call(s32[21]{0:T(128)} %get-tuple-element.239.block_ref, ...), custom_call_target="tpu_custom_call" | custom-call | tf_op jit(solution)/shard_map/pallas_call | solution.py:103
  424.0 12.6 shard_map.69
  444.0 91.3 %collective-permute-done.7.refs_3_ = bf16[1,128,1024]{2,1,0:T(8,128)(2,1)} collective-permute-done((bf16[1,128,1024]{2,1,0:T(8,128)(2,1)}, bf16[1,128,1024]{2,1,0:T(8,128)(2,1)}, u32[]{:S(2)}, u32[]{:S(2)}) %collective-permute-start.7) | collective-permute-done | bytes 262176 | tf_op jit(solution)/shard_map/ppermute | solution.py:16
  543.3 50.9 %collective-permute-done.9.refs_5_ = bf16[1,128,1024]{2,1,0:T(8,128)(2,1)} collective-permute-done((bf16[1,128,1024]{2,1,0:T(8,128)(2,1)}, bf16[1,128,1024]{2,1,0:T(8,128)(2,1)}, u32[]{:S(2)}, u32[]{:S(2)}) %collective-permute-start.9) | collective-permute-done | bytes 262176 | tf_op jit(solution)/shard_map/ppermute | solution.py:16
  607.2 19.8 %shard_map.71 = (bf16[8,128,1024]{2,1,0:T(8,128)(2,1)}, bf16[8,128,1024]{2,1,0:T(8,128)(2,1)}, bf16[8,128,1024]{2,1,0:T(8,128)(2,1)}) custom-call(s32[24]{0:T(128)} %get-tuple-element.235.block_ref, s32[24]{0:T(128)} %get-tuple-element.234.filled_ref, s32[1]{0:T(128)} %constant.203.clone.1.base_ref, bf16[128,128,1024]{2,1,0:T(8,128)(2,1)} %bitcast.150, ...), custom_call_target="tpu_custom_call" | custom-call | tf_op jit(solution)/shard_map/pallas_call | solution.py:103
  627.2 150.3 %collective-permute-done.21.refs_3_ = bf16[8,128,1024]{2,1,0:T(8,128)(2,1)} collective-permute-done((bf16[8,128,1024]{2,1,0:T(8,128)(2,1)}, bf16[8,128,1024]{2,1,0:T(8,128)(2,1)}, u32[]{:S(2)}, u32[]{:S(2)}) %collective-permute-start.21) | collective-permute-done | bytes 2097184 | tf_op jit(solution)/shard_map/ppermute | solution.py:16
  778.3 44.8 %collective-permute-start.27 = (bf16[8,128,1024]{2,1,0:T(8,128)(2,1)}, bf16[8,128,1024]{2,1,0:T(8,128)(2,1)}, u32[]{:S(2)}, u32[]{:S(2)}) collective-permute-start(bf16[8,128,1024]{2,1,0:T(8,128)(2,1)} %get-tuple-element.115), channel_id=1, source_target_pairs={{0,12},{4,8},{8,4},{12,0},{16,28},{20,24},{24,20},{28,16},{1,13},{... | collective-permute-start | bytes 6291464 | tf_op jit(solution)/shard_map/ppermute | solution.py:16
  824.6 18.2 %shard_map.72 = (bf16[6,128,1024]{2,1,0:T(8,128)(2,1)}, bf16[6,128,1024]{2,1,0:T(8,128)(2,1)}, bf16[6,128,1024]{2,1,0:T(8,128)(2,1)}, bf16[6,128,1024]{2,1,0:T(8,128)(2,1)}) custom-call(s32[24]{0:T(128)} %get-tuple-element.233.block_ref, s32[24]{0:T(128)} %get-tuple-element.232.filled_ref, s32[1]{0:T(128)} %constant.203.clone.1.base_ref, ...), custom_call_target="tpu_custom_call" | custom-call | tf_op jit(solution)/shard_map/pallas_call | solution.py:103
  844.2 66.8 %collective-permute-start.28 = (bf16[6,128,1024]{2,1,0:T(8,128)(2,1)}, bf16[6,128,1024]{2,1,0:T(8,128)(2,1)S(1)}, u32[]{:S(2)}, u32[]{:S(2)}) collective-permute-start(bf16[6,128,1024]{2,1,0:T(8,128)(2,1)} %get-tuple-element.116), channel_id=1, source_target_pairs={{0,16},{4,20},{8,24},{12,28},{16,0},{20,4},{24,8},{28,12},{1,17},{... | collective-permute-start | bytes 4718600 | tf_op jit(solution)/shard_map/ppermute | solution.py:16
  918.3 14.3 %shard_map.64.owned_ref = bf16[160,128,1024]{2,1,0:T(8,128)(2,1)} custom-call(s32[20]{0:T(128)} %get-tuple-element.245.block_ref, s32[20]{0:T(128)} %get-tuple-element.244.filled_ref, s32[1]{0:T(128)} %bitcast.41.base_ref, bf16[128,128,1024]{2,1,0:T(8,128)(2,1)} %bitcast.152, bf16[128,128,256]{2,1,0:T(8,128)(2,1)} %bitcast.158, ...), custom_call_target="tpu_custom_call" | custom-call | tf_op jit(solution)/shard_map/pallas_call | solution.py:103
  933.4 7.7 shard_map.68.owned_ref
  941.1 46.0 %shard_map.70 = bf16[160,128,1024]{2,1,0:T(8,128)(2,1)} custom-call(s32[56]{0:T(128)} %concatenate.65.slot_ref, bf16[160,128,1024]{2,1,0:T(8,128)(2,1)} %shard_map.68.owned_ref, bf16[8,128,1024]{2,1,0:T(8,128)(2,1)} %copy-done.5, bf16[8,128,1024]{2,1,0:T(8,128)(2,1)} %collective-permute-done.19.refs_1_, ...), custom_call_target="tpu_custom_call", output_to_operand_aliasing={{}: (1, {})} | custom-call | tf_op jit(solution)/shard_map/pallas_call | solution.py:142
  993.2 13.6 collective-permute-start.32
  1009.9 71.3 %collective-permute-done.28.rest_0_ = bf16[6,128,1024]{2,1,0:T(8,128)(2,1)S(1)} collective-permute-done((bf16[6,128,1024]{2,1,0:T(8,128)(2,1)}, bf16[6,128,1024]{2,1,0:T(8,128)(2,1)S(1)}, u32[]{:S(2)}, u32[]{:S(2)}) %collective-permute-start.28) | collective-permute-done | bytes 1572896 | tf_op jit(solution)/shard_map/ppermute | solution.py:16
  1082.9 31.4 %collective-permute-done.29.rest_1_ = bf16[6,128,1024]{2,1,0:T(8,128)(2,1)} collective-permute-done((bf16[6,128,1024]{2,1,0:T(8,128)(2,1)}, bf16[6,128,1024]{2,1,0:T(8,128)(2,1)}, u32[]{:S(2)}, u32[]{:S(2)}) %collective-permute-start.29) | collective-permute-done | bytes 1572896 | tf_op jit(solution)/shard_map/ppermute | solution.py:16
  1127.1 62.4 %collective-permute-start.33 = (bf16[3,128,1024]{2,1,0:T(8,128)(2,1)}, bf16[3,128,1024]{2,1,0:T(8,128)(2,1)}, u32[]{:S(2)}, u32[]{:S(2)}) collective-permute-start(bf16[3,128,1024]{2,1,0:T(8,128)(2,1)} %get-tuple-element.93), channel_id=1, source_target_pairs={{0,12},{4,8},{8,4},{12,0},{16,28},{20,24},{24,20},{28,16},{1,13},{... | collective-permute-start | bytes 2359304 | tf_op jit(solution)/shard_map/ppermute | solution.py:16
  1201.0 24.0 %collective-permute-done.33 = bf16[3,128,1024]{2,1,0:T(8,128)(2,1)} collective-permute-done((bf16[3,128,1024]{2,1,0:T(8,128)(2,1)}, bf16[3,128,1024]{2,1,0:T(8,128)(2,1)}, u32[]{:S(2)}, u32[]{:S(2)}) %collective-permute-start.33) | collective-permute-done | bytes 786464 | tf_op jit(solution)/shard_map/ppermute | solution.py:16
  1228.0 103.4 %collective-permute-done.35 = bf16[3,128,1024]{2,1,0:T(8,128)(2,1)} collective-permute-done((bf16[3,128,1024]{2,1,0:T(8,128)(2,1)}, bf16[3,128,1024]{2,1,0:T(8,128)(2,1)}, u32[]{:S(2)}, u32[]{:S(2)}) %collective-permute-start.35) | collective-permute-done | bytes 786464 | tf_op jit(solution)/shard_map/ppermute | solution.py:16
  1368.6 13.1 collective-permute-done.38
  (264 shorter events, 158.6 us)
Async XLA Ops:
  6.5 206.6 %all-gather.5.cloned.1.call-start = ((), (), s32[]{:S(2)}) async-start(), calls=%async_computation.2 | async-start | bytes 41943040 | tf_op jit(solution)/shard_map/all_gather | solution.py:311
  7.3 275.4 %all-reduce.7.cloned.1.call-start = ((), (), s32[]{:S(2)}) async-start(), calls=%async_computation.1 | async-start | bytes 1048576 | tf_op jit(solution)/shard_map/psum | solution.py:314
  10.1 370.9 %all-reduce.5.cloned.1.call-start = ((), (), s32[]{:S(2)}) async-start(), calls=%async_computation | async-start | bytes 2703360 | tf_op jit(solution)/shard_map/psum | solution.py:328
  264.3 669.1 %all-gather.7.cloned.1.call-start = ((), (), s32[]{:S(2)}) async-start(), calls=%async_computation.3 | async-start | bytes 10321920 | tf_op jit(solution)/shard_map/all_gather | solution.py:363
  276.4 131.7 %collective-permute-start.13 = (bf16[9,128,128]{2,1,0:T(8,128)(2,1)}, bf16[9,128,128]{2,1,0:T(8,128)(2,1)S(1)}, u32[]{:S(2)}, u32[]{:S(2)}) collective-permute-start(bf16[9,128,128]{2,1,0:T(8,128)(2,1)} %get-tuple-element.87), channel_id=1, source_target_pairs={{0,16},{4,20},{8,24},{12,28},{16,0},{20,4},{24,8},{28,12},{1,17},{... | collective-permute-start | bytes 884744 | tf_op jit(solution)/shard_map/ppermute | solution.py:16
  278.8 129.3 %collective-permute-start.14 = (bf16[9,128,128]{2,1,0:T(8,128)(2,1)}, bf16[9,128,128]{2,1,0:T(8,128)(2,1)S(1)}, u32[]{:S(2)}, u32[]{:S(2)}) collective-permute-start(bf16[9,128,128]{2,1,0:T(8,128)(2,1)} %get-tuple-element.88), channel_id=1, source_target_pairs={{0,20},{4,16},{8,28},{12,24},{16,4},{20,0},{24,12},{28,8},{1,21},{... | collective-permute-start | bytes 884744 | tf_op jit(solution)/shard_map/ppermute | solution.py:16
  436.6 166.7 %collective-permute-start.18 = (bf16[8,128,1024]{2,1,0:T(8,128)(2,1)}, bf16[8,128,1024]{2,1,0:T(8,128)(2,1)S(1)}, u32[]{:S(2)}, u32[]{:S(2)}) collective-permute-start(bf16[8,128,1024]{2,1,0:T(8,128)(2,1)} %get-tuple-element.106), channel_id=1, source_target_pairs={{0,8},{4,12},{8,0},{12,4},{16,24},{20,28},{24,16},{28,20},{1,9},{5... | collective-permute-start | bytes 6291464 | tf_op jit(solution)/shard_map/ppermute | solution.py:16
  438.4 167.2 %collective-permute-start.19 = (bf16[8,128,1024]{2,1,0:T(8,128)(2,1)}, bf16[8,128,1024]{2,1,0:T(8,128)(2,1)}, u32[]{:S(2)}, u32[]{:S(2)}) collective-permute-start(bf16[8,128,1024]{2,1,0:T(8,128)(2,1)} %get-tuple-element.107), channel_id=1, source_target_pairs={{0,12},{4,8},{8,4},{12,0},{16,28},{20,24},{24,20},{28,16},{1,13},{... | collective-permute-start | bytes 6291464 | tf_op jit(solution)/shard_map/ppermute | solution.py:16
  444.0 183.0 %collective-permute-start.20 = (bf16[8,128,1024]{2,1,0:T(8,128)(2,1)}, bf16[8,128,1024]{2,1,0:T(8,128)(2,1)}, u32[]{:S(2)}, u32[]{:S(2)}) collective-permute-start(bf16[8,128,1024]{2,1,0:T(8,128)(2,1)} %get-tuple-element.108), channel_id=1, source_target_pairs={{0,16},{4,20},{8,24},{12,28},{16,0},{20,4},{24,8},{28,12},{1,17},{... | collective-permute-start | bytes 6291464 | tf_op jit(solution)/shard_map/ppermute | solution.py:16
  543.2 234.4 %collective-permute-start.21 = (bf16[8,128,1024]{2,1,0:T(8,128)(2,1)}, bf16[8,128,1024]{2,1,0:T(8,128)(2,1)}, u32[]{:S(2)}, u32[]{:S(2)}) collective-permute-start(bf16[8,128,1024]{2,1,0:T(8,128)(2,1)} %get-tuple-element.109), channel_id=1, source_target_pairs={{0,20},{4,16},{8,28},{12,24},{16,4},{20,0},{24,12},{28,8},{1,21},{... | collective-permute-start | bytes 6291464 | tf_op jit(solution)/shard_map/ppermute | solution.py:16
  600.8 177.5 %collective-permute-start.22 = (bf16[8,128,1024]{2,1,0:T(8,128)(2,1)}, bf16[8,128,1024]{2,1,0:T(8,128)(2,1)}, u32[]{:S(2)}, u32[]{:S(2)}) collective-permute-start(bf16[8,128,1024]{2,1,0:T(8,128)(2,1)} %get-tuple-element.110), channel_id=1, source_target_pairs={{0,24},{4,28},{8,16},{12,20},{16,8},{20,12},{24,0},{28,4},{1,25},{... | collective-permute-start | bytes 6291464 | tf_op jit(solution)/shard_map/ppermute | solution.py:16
  603.3 240.9 %collective-permute-start.23 = (bf16[8,128,1024]{2,1,0:T(8,128)(2,1)}, bf16[8,128,1024]{2,1,0:T(8,128)(2,1)}, u32[]{:S(2)}, u32[]{:S(2)}) collective-permute-start(bf16[8,128,1024]{2,1,0:T(8,128)(2,1)} %get-tuple-element.111), channel_id=1, source_target_pairs={{0,28},{4,24},{8,20},{12,16},{16,12},{20,8},{24,4},{28,0},{1,29},{... | collective-permute-start | bytes 6291464 | tf_op jit(solution)/shard_map/ppermute | solution.py:16
  605.7 306.4 %collective-permute-start.24 = (bf16[8,128,1024]{2,1,0:T(8,128)(2,1)}, bf16[8,128,1024]{2,1,0:T(8,128)(2,1)}, u32[]{:S(2)}, u32[]{:S(2)}) collective-permute-start(bf16[8,128,1024]{2,1,0:T(8,128)(2,1)} %get-tuple-element.112), channel_id=1, source_target_pairs={{0,4},{4,0},{8,12},{12,8},{16,20},{20,16},{24,28},{28,24},{1,5},{5... | collective-permute-start | bytes 6291464 | tf_op jit(solution)/shard_map/ppermute | solution.py:16
  627.1 285.1 %collective-permute-start.25 = (bf16[8,128,1024]{2,1,0:T(8,128)(2,1)}, bf16[8,128,1024]{2,1,0:T(8,128)(2,1)}, u32[]{:S(2)}, u32[]{:S(2)}) collective-permute-start(bf16[8,128,1024]{2,1,0:T(8,128)(2,1)} %get-tuple-element.113), channel_id=1, source_target_pairs={{0,4},{4,0},{8,12},{12,8},{16,20},{20,16},{24,28},{28,24},{1,5},{5... | collective-permute-start | bytes 6291464 | tf_op jit(solution)/shard_map/ppermute | solution.py:16
  777.6 136.6 %collective-permute-start.26 = (bf16[8,128,1024]{2,1,0:T(8,128)(2,1)}, bf16[8,128,1024]{2,1,0:T(8,128)(2,1)}, u32[]{:S(2)}, u32[]{:S(2)}) collective-permute-start(bf16[8,128,1024]{2,1,0:T(8,128)(2,1)} %get-tuple-element.114), channel_id=1, source_target_pairs={{0,8},{4,12},{8,0},{12,4},{16,24},{20,28},{24,16},{28,20},{1,9},{5... | collective-permute-start | bytes 6291464 | tf_op jit(solution)/shard_map/ppermute | solution.py:16
  778.3 214.9 %collective-permute-start.27 = (bf16[8,128,1024]{2,1,0:T(8,128)(2,1)}, bf16[8,128,1024]{2,1,0:T(8,128)(2,1)}, u32[]{:S(2)}, u32[]{:S(2)}) collective-permute-start(bf16[8,128,1024]{2,1,0:T(8,128)(2,1)} %get-tuple-element.115), channel_id=1, source_target_pairs={{0,12},{4,8},{8,4},{12,0},{16,28},{20,24},{24,20},{28,16},{1,13},{... | collective-permute-start | bytes 6291464 | tf_op jit(solution)/shard_map/ppermute | solution.py:16
  844.2 237.0 %collective-permute-start.28 = (bf16[6,128,1024]{2,1,0:T(8,128)(2,1)}, bf16[6,128,1024]{2,1,0:T(8,128)(2,1)S(1)}, u32[]{:S(2)}, u32[]{:S(2)}) collective-permute-start(bf16[6,128,1024]{2,1,0:T(8,128)(2,1)} %get-tuple-element.116), channel_id=1, source_target_pairs={{0,16},{4,20},{8,24},{12,28},{16,0},{20,4},{24,8},{28,12},{1,17},{... | collective-permute-start | bytes 4718600 | tf_op jit(solution)/shard_map/ppermute | solution.py:16
  912.0 202.3 %collective-permute-start.29 = (bf16[6,128,1024]{2,1,0:T(8,128)(2,1)}, bf16[6,128,1024]{2,1,0:T(8,128)(2,1)}, u32[]{:S(2)}, u32[]{:S(2)}) collective-permute-start(bf16[6,128,1024]{2,1,0:T(8,128)(2,1)} %get-tuple-element.117), channel_id=1, source_target_pairs={{0,20},{4,16},{8,28},{12,24},{16,4},{20,0},{24,12},{28,8},{1,21},{... | collective-permute-start | bytes 4718600 | tf_op jit(solution)/shard_map/ppermute | solution.py:16
  912.2 205.3 %collective-permute-start.30 = (bf16[6,128,1024]{2,1,0:T(8,128)(2,1)}, bf16[6,128,1024]{2,1,0:T(8,128)(2,1)}, u32[]{:S(2)}, u32[]{:S(2)}) collective-permute-start(bf16[6,128,1024]{2,1,0:T(8,128)(2,1)} %get-tuple-element.118), channel_id=1, source_target_pairs={{0,24},{4,28},{8,16},{12,20},{16,8},{20,12},{24,0},{28,4},{1,25},{... | collective-permute-start | bytes 4718600 | tf_op jit(solution)/shard_map/ppermute | solution.py:16
  914.2 206.4 %collective-permute-start.31 = (bf16[6,128,1024]{2,1,0:T(8,128)(2,1)}, bf16[6,128,1024]{2,1,0:T(8,128)(2,1)}, u32[]{:S(2)}, u32[]{:S(2)}) collective-permute-start(bf16[6,128,1024]{2,1,0:T(8,128)(2,1)} %get-tuple-element.119), channel_id=1, source_target_pairs={{0,28},{4,24},{8,20},{12,16},{16,12},{20,8},{24,4},{28,0},{1,29},{... | collective-permute-start | bytes 4718600 | tf_op jit(solution)/shard_map/ppermute | solution.py:16
  993.2 206.0 %collective-permute-start.32 = (bf16[3,128,1024]{2,1,0:T(8,128)(2,1)}, bf16[3,128,1024]{2,1,0:T(8,128)(2,1)S(1)}, u32[]{:S(2)}, u32[]{:S(2)}) collective-permute-start(bf16[3,128,1024]{2,1,0:T(8,128)(2,1)} %get-tuple-element.92), channel_id=1, source_target_pairs={{0,8},{4,12},{8,0},{12,4},{16,24},{20,28},{24,16},{28,20},{1,9},{5... | collective-permute-start | bytes 2359304 | tf_op jit(solution)/shard_map/ppermute | solution.py:16
  1197.5 185.2 %collective-permute-start.39 = (bf16[8,128,1024]{2,1,0:T(8,128)(2,1)}, bf16[8,128,1024]{2,1,0:T(8,128)(2,1)S(1)}, u32[]{:S(2)}, u32[]{:S(2)}) collective-permute-start(bf16[8,128,1024]{2,1,0:T(8,128)(2,1)} %get-tuple-element.121), channel_id=1, source_target_pairs={{0,4},{4,0},{8,12},{12,8},{16,20},{20,16},{24,28},{28,24},{1,5},{5... | collective-permute-start | bytes 6291464 | tf_op jit(solution)/shard_map/ppermute | solution.py:16
  1197.5 185.1 %collective-permute-start.40 = (bf16[8,128,1024]{2,1,0:T(8,128)(2,1)}, bf16[8,128,1024]{2,1,0:T(8,128)(2,1)}, u32[]{:S(2)}, u32[]{:S(2)}) collective-permute-start(bf16[8,128,1024]{2,1,0:T(8,128)(2,1)} %get-tuple-element.122), channel_id=1, source_target_pairs={{0,8},{4,12},{8,0},{12,4},{16,24},{20,28},{24,16},{28,20},{1,9},{5... | collective-permute-start | bytes 6291464 | tf_op jit(solution)/shard_map/ppermute | solution.py:16
  1199.2 183.4 %collective-permute-start.41 = (bf16[8,128,1024]{2,1,0:T(8,128)(2,1)}, bf16[8,128,1024]{2,1,0:T(8,128)(2,1)}, u32[]{:S(2)}, u32[]{:S(2)}) collective-permute-start(bf16[8,128,1024]{2,1,0:T(8,128)(2,1)} %get-tuple-element.123), channel_id=1, source_target_pairs={{0,12},{4,8},{8,4},{12,0},{16,28},{20,24},{24,20},{28,16},{1,13},{... | collective-permute-start | bytes 6291464 | tf_op jit(solution)/shard_map/ppermute | solution.py:16
  (41 other events, 1628.7 us)
Sparse Core Ops, SparseCore 0:
  8.9 204.2 all-gather.4
  215.5 33.4 all-reduce.6
  264.4 116.5 all-reduce.4
  414.9 57.4 all-gather.6

commit v4 on v3

--- a/solution.py
+++ b/solution.py
@@ -283,8 +283,7 @@
     half = row_count // 2
     near, far = list(range(1, half)), list(range(half, row_count))
     order = near[half // 2 - 1 :] + far + near[: half // 2 - 1]
-    early_parts = [(0, max(1, early // 6))]
-    early_parts += [(early_parts[0][1], early - early_parts[0][1])]
+    classes = ((near, low), (far, early))
 
     owner_of = band_owner[:, 0]
     position = jnp.arange(block_count, dtype=jnp.int32)
@@ -303,10 +302,18 @@
 
     z = eigvecs.reshape(block_count, ROWS, width)
 
+    lead = max(1, early // 6)
     raw = {}
-    for at, count in early_parts:
-        packed = gather_blocks(z, *tables(at, count), len(order), count)
-        raw[at] = [swap(item, row_count, d) for d, item in zip(order, packed)]
+    packed = gather_blocks(z, *tables(0, lead), len(order), lead)
+    moved = {d: swap(item, row_count, d) for d, item in zip(order, packed)}
+    for number, (distances, until) in enumerate(classes):
+        raw[number] = [(0, lead, [moved[d] for d in distances])]
+    for number, (distances, until) in reversed(list(enumerate(classes))):
+        count = until - lead
+        if count:
+            packed = gather_blocks(z, *tables(lead, count, distances), len(distances), count)
+            packed = [swap(item, row_count, d) for d, item in zip(distances, packed)]
+            raw[number].append((lead, count, packed))
 
     candidates = lax.all_gather(reflectors, "col", axis=0)
     panels = [lax.dynamic_index_in_dim(candidates, owners[which], 0, keepdims=False) for which in range(2)]
@@ -335,8 +342,10 @@
 
     both = jnp.concatenate(panels, axis=1)
     slim = lax.dynamic_slice(both, (0, col * share), (both.shape[0], share)).reshape(block_count, ROWS, share)
-    slim_packed = gather_blocks(slim, *tables(0, early), len(order), early)
-    slim_list = [swap(item, row_count, d) for d, item in zip(order, slim_packed)]
+    slim_list = []
+    for distances, until in classes:
+        slim_packed = gather_blocks(slim, *tables(0, until, distances), len(distances), until)
+        slim_list += [swap(item, row_count, d) for d, item in zip(distances, slim_packed)]
 
     v0 = panels[0].reshape(block_count, ROWS, depth)
     v1 = panels[1].reshape(block_count, ROWS, depth)
@@ -356,17 +365,22 @@
     late["far"] = [swap(item, row_count, d) for d, item in zip(far, done)]
     done = finish_here(z, v0, v1, update, *tables(low, capacity - low, near), len(near), capacity - low)
     late["near"] = [swap(item, row_count, d) for d, item in zip(near, done)]
-    done = finish_here(z, v0, v1, update, *tables(early, low - early), len(order), low - early)
-    late["last"] = [swap(item, row_count, d) for d, item in zip(order, done)]
+    done = finish_here(z, v0, v1, update, *tables(early, low - early, far), len(far), low - early)
+    late["last"] = [swap(item, row_count, d) for d, item in zip(far, done)]
 
     slim_list, _ = lax.optimization_barrier((slim_list, done))
     wide_there = lax.all_gather(jnp.concatenate(slim_list, axis=0), "col", axis=0)
 
     mine = lax.dynamic_slice(slot_table, (0, me * capacity), (2, capacity))
     (owned,) = finish_here(z, v0, v1, update, mine[0], mine[1], 1, capacity, me * capacity, slot_total)
-    for at, count in early_parts:
-        slots = jnp.concatenate([(me ^ d) * capacity + at + jnp.arange(count, dtype=jnp.int32) for d in order])
-        owned = settle_there(owned, raw[at], wide_there, update, at, early, slots)
+    offset = 0
+    for number, (distances, until) in enumerate(classes):
+        for at, count, items in raw[number]:
+            slots = [(me ^ d) * capacity + at + jnp.arange(count, dtype=jnp.int32) for d in distances]
+            owned = settle_there(
+                owned, items, wide_there, update, offset + at, until, jnp.concatenate(slots)
+            )
+        offset += len(distances) * until
 
     def place(owned, distance, at, value):
         return lax.dynamic_update_slice(owned, value, ((me ^ distance) * capacity + at, 0, 0))
@@ -377,14 +391,23 @@
         hits, fits = jax.vmap(lambda c: match_spares(c, low, base, capacity))(crossing)
         fits = jnp.all(fits)
         seen = [lax.dynamic_index_in_dim(hits, me ^ d, 0, keepdims=False) for d in far]
-        index, filled = [], []
-        for d in near:
-            for stream in range(len(far)):
-                found = seen[stream][stream, :, (far[stream] ^ d) - half, :]
-                index.append(jnp.sum(found * jnp.arange(base - low)[:, None], axis=0))
-                filled.append(jnp.sum(found, axis=0))
-        relayed = relay_blocks(late["far"], jnp.concatenate(index), jnp.concatenate(filled), len(near), overflow)
-        relayed = [swap(item, row_count, d) for d, item in zip(near, relayed)]
+        lanes = len(far) // 2
+        relayed = []
+        for part in range(2):
+            index, filled = [], []
+            for d in near:
+                for stream in range(part * lanes, (part + 1) * lanes):
+                    found = seen[stream][stream, :, (far[stream] ^ d) - half, :]
+                    index.append(jnp.sum(found * jnp.arange(base - low)[:, None], axis=0))
+                    filled.append(jnp.sum(found, axis=0))
+            sent = relay_blocks(
+                late["far"][part * lanes : (part + 1) * lanes],
+                jnp.concatenate(index),
+                jnp.concatenate(filled),
+                len(near),
+                overflow,
+            )
+            relayed += [swap(item, row_count, d) for d, item in zip(near, sent)]
 
     for d, item in zip(near, late["near"]):
         owned = place(owned, d, low, item)
@@ -406,7 +429,7 @@
             return [jnp.zeros((overflow, ROWS, width), z.dtype)] * len(far)
 
         straight = lax.cond(gate, nothing, direct)
-    for d, item in zip(order, late["last"]):
+    for d, item in zip(far, late["last"]):
         owned = place(owned, d, early, item)
 
     if overflow:
@@ -416,9 +439,9 @@
                 options, picked = [], 0
                 for number, step in enumerate(near):
                     stream = (d ^ step) - half
-                    options.append((number, stream * overflow + item))
+                    options.append((stream // lanes * len(near) + number, stream % lanes * overflow + item))
                     picked = picked + (number + 1) * jnp.sum(seen[owner][stream, :, owner, item])
-                options.append((len(near) + owner, item))
+                options.append((len(relayed) + owner, item))
                 origins.append(tuple(options))
                 choice.append(jnp.where(fits, picked, len(options)))
                 slots.append((me ^ d) * capacity + base + item)

time: 1400 us -> 1380 us (0.986)
  starting transfers between devices: 231 us -> 125 us
  waiting for transfers between devices: 840 us -> 923 us
    ppermute x38, starting transfers between devices: 231 us -> 125 us  [swap(): lax.ppermute(value, 'row', [(s, s ^ distance) for s in range(row_count)])]
    ppermute x38, waiting for transfers between devices: 544 us -> 639 us  [swap(): lax.ppermute(value, 'row', [(s, s ^ distance) for s in range(row_count)])]
    pallas_call x2 -> x4, Pallas kernels: 53.6 us -> 64.1 us  [settle_there(): pl.pallas_call(functools.partial(settle_kernel, groups, count), grid_spec...]
  transfers between devices with their start and end apart: 42 -> 42, of which waited for: 13 -> 11; matrix products, arithmetic and copies ran while one was open for 8% -> 8% of each run, Pallas kernels for 11% -> 12%
where the time goes in v4:
time: 1380 us
  waiting for transfers between devices  923 us (67%)
  Pallas kernels  162 us (12%)
  starting transfers between devices  125 us (9%)
  local copies, waits for them, and re-layouts  52.2 us (4%)
  matrix products  41.6 us (3%)
  between operations  39.5 us (3%)
  other arithmetic  35.4 us (3%)
    ppermute x38, waiting for transfers between devices, swap(): lax.ppermute(value, 'row', [(s, s ^ distance) for s in range(row_count)])  639 us
    all_gather x1, waiting for transfers between devices, body(): candidates = lax.all_gather(reflectors, 'col', axis=0)  196 us
    ppermute x38, starting transfers between devices, swap(): lax.ppermute(value, 'row', [(s, s ^ distance) for s in range(row_count)])  125 us
    psum x1, waiting for transfers between devices, body(): lax.psum(jnp.concatenate([partial_value, told], axis=0), 'row')  86.7 us
    pallas_call x4, Pallas kernels, settle_there(): pl.pallas_call(functools.partial(settle_kernel, groups, count), grid_spec...  64.1 us
    pallas_call x4, Pallas kernels, finish_here(): pl.pallas_call(functools.partial(finish_kernel, groups, count), grid_spec...  63.2 us
    dot_general x2, matrix products, body(): lax.dot_general(panel, eigvecs, contract_rows, preferred_element_type=jnp...  35.2 us
  transfers between devices with their start and end apart: 42, of which 11 were waited for; matrix products, arithmetic and copies ran while one was open for 8% of the time, Pallas kernels for 12%

profile of v4, /device:TPU:0, one launch (start us, length us, event | category | flops | bytes accessed | tf_op | source)
XLA Modules:
  0.0 1379.2 jit_solution(6869790229043257064)
XLA Ops:
  17.0 196.2 %all-gather.5.cloned.1.call-done = bf16[65536,256]{1,0:T(8,128)(2,1)} async-done(((bf16[16384,256]{1,0:T(8,128)(2,1)}), bf16[65536,256]{1,0:T(8,128)(2,1)}) %all-gather.5.cloned.1.call-update) | async-done | bytes 33554448 | tf_op jit(solution)/shard_map/all_gather | solution.py:318
  213.2 6.5 constant_dynamic-slice_fusion.83
  228.0 17.7 %convolution_convert_fusion.2 = bf16[256,1024]{1,0:T(8,128)(2,1)S(1)} fusion(bf16[16384,1024]{1,0:T(8,128)(2,1)} %param.8, bf16[1,16384,256]{2,1,0:T(8,128)(2,1)} %copy-done.1), kind=kOutput, calls=%fused_computation.26 | convolution fusion | flops 8590196736 | bytes 42467328 | tf_op jit(solution)/shard_map/dot_general | solution.py:325
  245.7 17.5 %convolution_convert_fusion.3 = bf16[256,1024]{1,0:T(8,128)(2,1)S(1)} fusion(bf16[16384,1024]{1,0:T(8,128)(2,1)} %param.8, bf16[1,16384,256]{2,1,0:T(8,128)(2,1)} %copy-done), kind=kOutput, calls=%fused_computation.27 | convolution fusion | flops 8590196736 | bytes 42467328 | tf_op jit(solution)/shard_map/dot_general | solution.py:325
  283.3 86.7 %all-reduce.5.cloned.1.call-done = bf16[528,1280]{1,0:T(8,128)(2,1)} async-done(((bf16[528,1280]{1,0:T(8,128)(2,1)}), bf16[528,1280]{1,0:T(8,128)(2,1)}) %all-reduce.5.cloned.1.call-update) | async-done | bytes 1351696 | tf_op jit(solution)/shard_map/psum | solution.py:335
  380.7 11.0 shard_map.68
  404.1 11.1 collective-permute-start.5
  416.9 8.3 shard_map.73
  440.2 190.8 %collective-permute-done.17.refs_0_ = bf16[1,128,1024]{2,1,0:T(8,128)(2,1)} collective-permute-done((bf16[1,128,1024]{2,1,0:T(8,128)(2,1)}, bf16[1,128,1024]{2,1,0:T(8,128)(2,1)}, u32[]{:S(2)}, u32[]{:S(2)}) %collective-permute-start.17) | collective-permute-done | bytes 262176 | tf_op jit(solution)/shard_map/ppermute | solution.py:16
  634.9 8.0 shard_map.70
  661.5 19.7 %shard_map.75 = (bf16[8,128,1024]{2,1,0:T(8,128)(2,1)}, bf16[8,128,1024]{2,1,0:T(8,128)(2,1)}, bf16[8,128,1024]{2,1,0:T(8,128)(2,1)}) custom-call(s32[24]{0:T(128)} %get-tuple-element.232.block_ref, s32[24]{0:T(128)} %get-tuple-element.231.filled_ref, s32[1]{0:T(128)} %constant.200.clone.1.base_ref, bf16[128,128,1024]{2,1,0:T(8,128)(2,1)} %bitcast.159, ...), custom_call_target="tpu_custom_call" | custom-call | tf_op jit(solution)/shard_map/pallas_call | solution.py:103
  681.2 18.2 %shard_map.76 = (bf16[6,128,1024]{2,1,0:T(8,128)(2,1)}, bf16[6,128,1024]{2,1,0:T(8,128)(2,1)}, bf16[6,128,1024]{2,1,0:T(8,128)(2,1)}, bf16[6,128,1024]{2,1,0:T(8,128)(2,1)}) custom-call(s32[24]{0:T(128)} %get-tuple-element.230.block_ref, s32[24]{0:T(128)} %get-tuple-element.229.filled_ref, s32[1]{0:T(128)} %constant.200.clone.1.base_ref, ...), custom_call_target="tpu_custom_call" | custom-call | tf_op jit(solution)/shard_map/pallas_call | solution.py:103
  700.4 155.3 %collective-permute-done.23.refs_2_ = bf16[8,128,1024]{2,1,0:T(8,128)(2,1)} collective-permute-done((bf16[8,128,1024]{2,1,0:T(8,128)(2,1)}, bf16[8,128,1024]{2,1,0:T(8,128)(2,1)}, u32[]{:S(2)}, u32[]{:S(2)}) %collective-permute-start.23) | collective-permute-done | bytes 2097184 | tf_op jit(solution)/shard_map/ppermute | solution.py:16
  857.9 40.8 %collective-permute-done.24.refs_3_ = bf16[8,128,1024]{2,1,0:T(8,128)(2,1)} collective-permute-done((bf16[8,128,1024]{2,1,0:T(8,128)(2,1)}, bf16[8,128,1024]{2,1,0:T(8,128)(2,1)}, u32[]{:S(2)}, u32[]{:S(2)}) %collective-permute-start.24) | collective-permute-done | bytes 2097184 | tf_op jit(solution)/shard_map/ppermute | solution.py:16
  908.9 57.3 %collective-permute-done.28.rest_0_ = bf16[6,128,1024]{2,1,0:T(8,128)(2,1)S(1)} collective-permute-done((bf16[6,128,1024]{2,1,0:T(8,128)(2,1)}, bf16[6,128,1024]{2,1,0:T(8,128)(2,1)S(1)}, u32[]{:S(2)}, u32[]{:S(2)}) %collective-permute-start.28) | collective-permute-done | bytes 1572896 | tf_op jit(solution)/shard_map/ppermute | solution.py:16
  969.8 87.7 %collective-permute-done.29.rest_1_ = bf16[6,128,1024]{2,1,0:T(8,128)(2,1)} collective-permute-done((bf16[6,128,1024]{2,1,0:T(8,128)(2,1)}, bf16[6,128,1024]{2,1,0:T(8,128)(2,1)}, u32[]{:S(2)}, u32[]{:S(2)}) %collective-permute-start.29) | collective-permute-done | bytes 1572896 | tf_op jit(solution)/shard_map/ppermute | solution.py:16
  1060.1 14.3 %shard_map.64.owned_ref = bf16[160,128,1024]{2,1,0:T(8,128)(2,1)} custom-call(s32[20]{0:T(128)} %get-tuple-element.246.block_ref, s32[20]{0:T(128)} %get-tuple-element.245.filled_ref, s32[1]{0:T(128)} %bitcast.41.base_ref, bf16[128,128,1024]{2,1,0:T(8,128)(2,1)} %bitcast.161, bf16[128,128,256]{2,1,0:T(8,128)(2,1)} %bitcast.167, ...), custom_call_target="tpu_custom_call" | custom-call | tf_op jit(solution)/shard_map/pallas_call | solution.py:103
  1084.3 27.7 %shard_map.71.owned_ref = bf16[160,128,1024]{2,1,0:T(8,128)(2,1)} custom-call(s32[33]{0:T(128)} %pad_add_fusion.12.slot_ref, bf16[160,128,1024]{2,1,0:T(8,128)(2,1)} %shard_map.69.owned_ref, bf16[11,128,1024]{2,1,0:T(8,128)(2,1)} %collective-permute-done.14.refs_0_, ...), custom_call_target="tpu_custom_call", output_to_operand_aliasing={{}: (1, {})} | custom-call | tf_op jit(solution)/shard_map/pallas_call | solution.py:142
  1117.1 26.9 %shard_map.74 = bf16[160,128,1024]{2,1,0:T(8,128)(2,1)} custom-call(s32[32]{0:T(128)} %pad_add_fusion.10.slot_ref, bf16[160,128,1024]{2,1,0:T(8,128)(2,1)} %shard_map.72.owned_ref, bf16[8,128,1024]{2,1,0:T(8,128)(2,1)} %copy-done.7, bf16[8,128,1024]{2,1,0:T(8,128)(2,1)} %collective-permute-done.22.refs_1_, ...), custom_call_target="tpu_custom_call", output_to_operand_aliasing={{}: (1, {})} | custom-call | tf_op jit(solution)/shard_map/pallas_call | solution.py:142
  1166.2 7.2 collective-permute-start.32
  1184.2 75.3 %collective-permute-done.32 = bf16[3,128,1024]{2,1,0:T(8,128)(2,1)S(1)} collective-permute-done((bf16[3,128,1024]{2,1,0:T(8,128)(2,1)}, bf16[3,128,1024]{2,1,0:T(8,128)(2,1)S(1)}, u32[]{:S(2)}, u32[]{:S(2)}) %collective-permute-start.32) | collective-permute-done | bytes 786464 | tf_op jit(solution)/shard_map/ppermute | solution.py:16
  1260.4 16.4 %collective-permute-done.33 = bf16[3,128,1024]{2,1,0:T(8,128)(2,1)S(1)} collective-permute-done((bf16[3,128,1024]{2,1,0:T(8,128)(2,1)}, bf16[3,128,1024]{2,1,0:T(8,128)(2,1)S(1)}, u32[]{:S(2)}, u32[]{:S(2)}) %collective-permute-start.33) | collective-permute-done | bytes 786464 | tf_op jit(solution)/shard_map/ppermute | solution.py:16
  1279.6 45.0 %collective-permute-start.40 = (bf16[4,128,1024]{2,1,0:T(8,128)(2,1)}, bf16[4,128,1024]{2,1,0:T(8,128)(2,1)}, u32[]{:S(2)}, u32[]{:S(2)}) collective-permute-start(bf16[4,128,1024]{2,1,0:T(8,128)(2,1)} %get-tuple-element.122), channel_id=1, source_target_pairs={{0,8},{4,12},{8,0},{12,4},{16,24},{20,28},{24,16},{28,20},{1,9},{5... | collective-permute-start | bytes 3145736 | tf_op jit(solution)/shard_map/ppermute | solution.py:16
  1356.0 14.5 %collective-permute-done.41.rest_5_ = bf16[4,128,1024]{2,1,0:T(8,128)(2,1)} collective-permute-done((bf16[4,128,1024]{2,1,0:T(8,128)(2,1)}, bf16[4,128,1024]{2,1,0:T(8,128)(2,1)}, u32[]{:S(2)}, u32[]{:S(2)}) %collective-permute-start.41) | collective-permute-done | bytes 1048608 | tf_op jit(solution)/shard_map/ppermute | solution.py:16
  (310 shorter events, 180.0 us)
Async XLA Ops:
  6.5 206.7 %all-gather.5.cloned.1.call-start = ((), (), s32[]{:S(2)}) async-start(), calls=%async_computation.2 | async-start | bytes 41943040 | tf_op jit(solution)/shard_map/all_gather | solution.py:318
  7.3 276.0 %all-reduce.7.cloned.1.call-start = ((), (), s32[]{:S(2)}) async-start(), calls=%async_computation.1 | async-start | bytes 1048576 | tf_op jit(solution)/shard_map/psum | solution.py:321
  10.1 359.8 %all-reduce.5.cloned.1.call-start = ((), (), s32[]{:S(2)}) async-start(), calls=%async_computation | async-start | bytes 2703360 | tf_op jit(solution)/shard_map/psum | solution.py:335
  264.4 815.5 %all-gather.7.cloned.1.call-start = ((), (), s32[]{:S(2)}) async-start(), calls=%async_computation.3 | async-start | bytes 11796480 | tf_op jit(solution)/shard_map/all_gather | solution.py:372
  272.5 120.2 %collective-permute-start.7 = (bf16[12,128,128]{2,1,0:T(8,128)(2,1)}, bf16[12,128,128]{2,1,0:T(8,128)(2,1)S(1)}, u32[]{:S(2)}, u32[]{:S(2)}) collective-permute-start(bf16[12,128,128]{2,1,0:T(8,128)(2,1)} %get-tuple-element.81), channel_id=1, source_target_pairs={{0,4},{4,0},{8,12},{12,8},{16,20},{20,16},{24,28},{28,24},{1,5},{5... | collective-permute-start | bytes 1179656 | tf_op jit(solution)/shard_map/ppermute | solution.py:16
  274.1 118.7 %collective-permute-start.8 = (bf16[12,128,128]{2,1,0:T(8,128)(2,1)}, bf16[12,128,128]{2,1,0:T(8,128)(2,1)S(1)}, u32[]{:S(2)}, u32[]{:S(2)}) collective-permute-start(bf16[12,128,128]{2,1,0:T(8,128)(2,1)} %get-tuple-element.82), channel_id=1, source_target_pairs={{0,8},{4,12},{8,0},{12,4},{16,24},{20,28},{24,16},{28,20},{1,9},{5... | collective-permute-start | bytes 1179656 | tf_op jit(solution)/shard_map/ppermute | solution.py:16
  275.5 117.2 %collective-permute-start.9 = (bf16[12,128,128]{2,1,0:T(8,128)(2,1)}, bf16[12,128,128]{2,1,0:T(8,128)(2,1)S(1)}, u32[]{:S(2)}, u32[]{:S(2)}) collective-permute-start(bf16[12,128,128]{2,1,0:T(8,128)(2,1)} %get-tuple-element.83), channel_id=1, source_target_pairs={{0,12},{4,8},{8,4},{12,0},{16,28},{20,24},{24,20},{28,16},{1,13},{... | collective-permute-start | bytes 1179656 | tf_op jit(solution)/shard_map/ppermute | solution.py:16
  425.2 229.3 %collective-permute-start.21 = (bf16[8,128,1024]{2,1,0:T(8,128)(2,1)}, bf16[8,128,1024]{2,1,0:T(8,128)(2,1)S(1)}, u32[]{:S(2)}, u32[]{:S(2)}) collective-permute-start(bf16[8,128,1024]{2,1,0:T(8,128)(2,1)} %get-tuple-element.106), channel_id=1, source_target_pairs={{0,16},{4,20},{8,24},{12,28},{16,0},{20,4},{24,8},{28,12},{1,17},{... | collective-permute-start | bytes 6291464 | tf_op jit(solution)/shard_map/ppermute | solution.py:16
  428.0 229.1 %collective-permute-start.22 = (bf16[8,128,1024]{2,1,0:T(8,128)(2,1)}, bf16[8,128,1024]{2,1,0:T(8,128)(2,1)}, u32[]{:S(2)}, u32[]{:S(2)}) collective-permute-start(bf16[8,128,1024]{2,1,0:T(8,128)(2,1)} %get-tuple-element.107), channel_id=1, source_target_pairs={{0,20},{4,16},{8,28},{12,24},{16,4},{20,0},{24,12},{28,8},{1,21},{... | collective-permute-start | bytes 6291464 | tf_op jit(solution)/shard_map/ppermute | solution.py:16
  434.2 196.8 %collective-permute-start.17 = (bf16[1,128,1024]{2,1,0:T(8,128)(2,1)}, bf16[1,128,1024]{2,1,0:T(8,128)(2,1)}, u32[]{:S(2)}, u32[]{:S(2)}) collective-permute-start(bf16[1,128,1024]{2,1,0:T(8,128)(2,1)} %get-tuple-element.102), channel_id=1, source_target_pairs={{0,16},{4,20},{8,24},{12,28},{16,0},{20,4},{24,8},{28,12},{1,17},{... | collective-permute-start | bytes 786440 | tf_op jit(solution)/shard_map/ppermute | solution.py:16
  436.8 206.1 %collective-permute-start.18 = (bf16[1,128,1024]{2,1,0:T(8,128)(2,1)}, bf16[1,128,1024]{2,1,0:T(8,128)(2,1)}, u32[]{:S(2)}, u32[]{:S(2)}) collective-permute-start(bf16[1,128,1024]{2,1,0:T(8,128)(2,1)} %get-tuple-element.103), channel_id=1, source_target_pairs={{0,20},{4,16},{8,28},{12,24},{16,4},{20,0},{24,12},{28,8},{1,21},{... | collective-permute-start | bytes 786440 | tf_op jit(solution)/shard_map/ppermute | solution.py:16
  437.5 207.0 %collective-permute-start.19 = (bf16[1,128,1024]{2,1,0:T(8,128)(2,1)}, bf16[1,128,1024]{2,1,0:T(8,128)(2,1)}, u32[]{:S(2)}, u32[]{:S(2)}) collective-permute-start(bf16[1,128,1024]{2,1,0:T(8,128)(2,1)} %get-tuple-element.104), channel_id=1, source_target_pairs={{0,24},{4,28},{8,16},{12,20},{16,8},{20,12},{24,0},{28,4},{1,25},{... | collective-permute-start | bytes 786440 | tf_op jit(solution)/shard_map/ppermute | solution.py:16
  642.9 256.2 %collective-permute-start.14 = (bf16[11,128,1024]{2,1,0:T(8,128)(2,1)}, bf16[11,128,1024]{2,1,0:T(8,128)(2,1)}, u32[]{:S(2)}, u32[]{:S(2)}) collective-permute-start(bf16[11,128,1024]{2,1,0:T(8,128)(2,1)} %get-tuple-element.99), channel_id=1, source_target_pairs={{0,4},{4,0},{8,12},{12,8},{16,20},{20,16},{24,28},{28,24},{1,5},{5... | collective-permute-start | bytes 8650760 | tf_op jit(solution)/shard_map/ppermute | solution.py:16
  644.5 256.7 %collective-permute-start.15 = (bf16[11,128,1024]{2,1,0:T(8,128)(2,1)}, bf16[11,128,1024]{2,1,0:T(8,128)(2,1)}, u32[]{:S(2)}, u32[]{:S(2)}) collective-permute-start(bf16[11,128,1024]{2,1,0:T(8,128)(2,1)} %get-tuple-element.100), channel_id=1, source_target_pairs={{0,8},{4,12},{8,0},{12,4},{16,24},{20,28},{24,16},{28,20},{1,9},{5... | collective-permute-start | bytes 8650760 | tf_op jit(solution)/shard_map/ppermute | solution.py:16
  648.4 253.5 %collective-permute-start.16 = (bf16[11,128,1024]{2,1,0:T(8,128)(2,1)}, bf16[11,128,1024]{2,1,0:T(8,128)(2,1)}, u32[]{:S(2)}, u32[]{:S(2)}) collective-permute-start(bf16[11,128,1024]{2,1,0:T(8,128)(2,1)} %get-tuple-element.101), channel_id=1, source_target_pairs={{0,12},{4,8},{8,4},{12,0},{16,28},{20,24},{24,20},{28,16},{1,13},{... | collective-permute-start | bytes 8650760 | tf_op jit(solution)/shard_map/ppermute | solution.py:16
  654.5 201.1 %collective-permute-start.23 = (bf16[8,128,1024]{2,1,0:T(8,128)(2,1)}, bf16[8,128,1024]{2,1,0:T(8,128)(2,1)}, u32[]{:S(2)}, u32[]{:S(2)}) collective-permute-start(bf16[8,128,1024]{2,1,0:T(8,128)(2,1)} %get-tuple-element.108), channel_id=1, source_target_pairs={{0,24},{4,28},{8,16},{12,20},{16,8},{20,12},{24,0},{28,4},{1,25},{... | collective-permute-start | bytes 6291464 | tf_op jit(solution)/shard_map/ppermute | solution.py:16
  657.1 241.5 %collective-permute-start.24 = (bf16[8,128,1024]{2,1,0:T(8,128)(2,1)}, bf16[8,128,1024]{2,1,0:T(8,128)(2,1)}, u32[]{:S(2)}, u32[]{:S(2)}) collective-permute-start(bf16[8,128,1024]{2,1,0:T(8,128)(2,1)} %get-tuple-element.109), channel_id=1, source_target_pairs={{0,28},{4,24},{8,20},{12,16},{16,12},{20,8},{24,4},{28,0},{1,29},{... | collective-permute-start | bytes 6291464 | tf_op jit(solution)/shard_map/ppermute | solution.py:16
  855.6 288.5 %collective-permute-start.25 = (bf16[8,128,1024]{2,1,0:T(8,128)(2,1)}, bf16[8,128,1024]{2,1,0:T(8,128)(2,1)}, u32[]{:S(2)}, u32[]{:S(2)}) collective-permute-start(bf16[8,128,1024]{2,1,0:T(8,128)(2,1)} %get-tuple-element.110), channel_id=1, source_target_pairs={{0,4},{4,0},{8,12},{12,8},{16,20},{20,16},{24,28},{28,24},{1,5},{5... | collective-permute-start | bytes 6291464 | tf_op jit(solution)/shard_map/ppermute | solution.py:16
  899.2 250.2 %collective-permute-start.26 = (bf16[8,128,1024]{2,1,0:T(8,128)(2,1)}, bf16[8,128,1024]{2,1,0:T(8,128)(2,1)}, u32[]{:S(2)}, u32[]{:S(2)}) collective-permute-start(bf16[8,128,1024]{2,1,0:T(8,128)(2,1)} %get-tuple-element.111), channel_id=1, source_target_pairs={{0,8},{4,12},{8,0},{12,4},{16,24},{20,28},{24,16},{28,20},{1,9},{5... | collective-permute-start | bytes 6291464 | tf_op jit(solution)/shard_map/ppermute | solution.py:16
  901.2 251.3 %collective-permute-start.27 = (bf16[8,128,1024]{2,1,0:T(8,128)(2,1)}, bf16[8,128,1024]{2,1,0:T(8,128)(2,1)}, u32[]{:S(2)}, u32[]{:S(2)}) collective-permute-start(bf16[8,128,1024]{2,1,0:T(8,128)(2,1)} %get-tuple-element.112), channel_id=1, source_target_pairs={{0,12},{4,8},{8,4},{12,0},{16,28},{20,24},{24,20},{28,16},{1,13},{... | collective-permute-start | bytes 6291464 | tf_op jit(solution)/shard_map/ppermute | solution.py:16
  901.8 155.6 %collective-permute-start.29 = (bf16[6,128,1024]{2,1,0:T(8,128)(2,1)}, bf16[6,128,1024]{2,1,0:T(8,128)(2,1)}, u32[]{:S(2)}, u32[]{:S(2)}) collective-permute-start(bf16[6,128,1024]{2,1,0:T(8,128)(2,1)} %get-tuple-element.114), channel_id=1, source_target_pairs={{0,20},{4,16},{8,28},{12,24},{16,4},{20,0},{24,12},{28,8},{1,21},{... | collective-permute-start | bytes 4718600 | tf_op jit(solution)/shard_map/ppermute | solution.py:16
  967.4 193.1 %collective-permute-start.30 = (bf16[6,128,1024]{2,1,0:T(8,128)(2,1)}, bf16[6,128,1024]{2,1,0:T(8,128)(2,1)S(1)}, u32[]{:S(2)}, u32[]{:S(2)}) collective-permute-start(bf16[6,128,1024]{2,1,0:T(8,128)(2,1)} %get-tuple-element.115), channel_id=1, source_target_pairs={{0,24},{4,28},{8,16},{12,20},{16,8},{20,12},{24,0},{28,4},{1,25},{... | collective-permute-start | bytes 4718600 | tf_op jit(solution)/shard_map/ppermute | solution.py:16
  1057.4 104.7 %collective-permute-start.31 = (bf16[6,128,1024]{2,1,0:T(8,128)(2,1)}, bf16[6,128,1024]{2,1,0:T(8,128)(2,1)}, u32[]{:S(2)}, u32[]{:S(2)}) collective-permute-start(bf16[6,128,1024]{2,1,0:T(8,128)(2,1)} %get-tuple-element.116), channel_id=1, source_target_pairs={{0,28},{4,24},{8,20},{12,16},{16,12},{20,8},{24,4},{28,0},{1,29},{... | collective-permute-start | bytes 4718600 | tf_op jit(solution)/shard_map/ppermute | solution.py:16
  1144.1 180.5 %collective-permute-start.36 = (bf16[4,128,1024]{2,1,0:T(8,128)(2,1)}, bf16[4,128,1024]{2,1,0:T(8,128)(2,1)}, u32[]{:S(2)}, u32[]{:S(2)}) collective-permute-start(bf16[4,128,1024]{2,1,0:T(8,128)(2,1)} %get-tuple-element.118), channel_id=1, source_target_pairs={{0,4},{4,0},{8,12},{12,8},{16,20},{20,16},{24,28},{28,24},{1,5},{5... | collective-permute-start | bytes 3145736 | tf_op jit(solution)/shard_map/ppermute | solution.py:16
  (60 other events, 1963.4 us)
Sparse Core Ops, SparseCore 0:
  8.9 204.2 all-gather.4
  215.5 33.3 all-reduce.6
  264.5 105.3 all-reduce.4
  399.7 72.5 all-gather.6

commit v5 on v4

--- a/solution.py
+++ b/solution.py
@@ -391,17 +391,17 @@
         hits, fits = jax.vmap(lambda c: match_spares(c, low, base, capacity))(crossing)
         fits = jnp.all(fits)
         seen = [lax.dynamic_index_in_dim(hits, me ^ d, 0, keepdims=False) for d in far]
-        lanes = len(far) // 2
+        cut = len(far) - max(1, len(far) // 4)
         relayed = []
-        for part in range(2):
+        for part, (start, stop) in enumerate(((0, cut), (cut, len(far)))):
             index, filled = [], []
             for d in near:
-                for stream in range(part * lanes, (part + 1) * lanes):
+                for stream in range(start, stop):
                     found = seen[stream][stream, :, (far[stream] ^ d) - half, :]
                     index.append(jnp.sum(found * jnp.arange(base - low)[:, None], axis=0))
                     filled.append(jnp.sum(found, axis=0))
             sent = relay_blocks(
-                late["far"][part * lanes : (part + 1) * lanes],
+                late["far"][start:stop],
                 jnp.concatenate(index),
                 jnp.concatenate(filled),
                 len(near),
@@ -439,7 +439,8 @@
                 options, picked = [], 0
                 for number, step in enumerate(near):
                     stream = (d ^ step) - half
-                    options.append((stream // lanes * len(near) + number, stream % lanes * overflow + item))
+                    part, lane = (0, stream) if stream < cut else (1, stream - cut)
+                    options.append((part * len(near) + number, lane * overflow + item))
                     picked = picked + (number + 1) * jnp.sum(seen[owner][stream, :, owner, item])
                 options.append((len(relayed) + owner, item))
                 origins.append(tuple(options))

time: 1380 us -> 1410 us (1.022)
  starting transfers between devices: 125 us -> 417 us
  waiting for transfers between devices: 923 us -> 649 us
    ppermute x38, starting transfers between devices: 125 us -> 416 us  [swap(): lax.ppermute(value, 'row', [(s, s ^ distance) for s in range(row_count)])]
    ppermute x38, waiting for transfers between devices: 639 us -> 365 us  [swap(): lax.ppermute(value, 'row', [(s, s ^ distance) for s in range(row_count)])]
  transfers between devices with their start and end apart: 42 -> 42, of which waited for: 11 -> 11; matrix products, arithmetic and copies ran while one was open for 8% -> 9% of each run, Pallas kernels for 12% -> 11%
where the time goes in v5:
time: 1410 us; the launch traced here: 1400 us
  waiting for transfers between devices  649 us (46%)
  starting transfers between devices  417 us (30%)
  Pallas kernels  162 us (11%)
  local copies, waits for them, and re-layouts  52.5 us (4%)
  matrix products  41.6 us (3%)
  other arithmetic  39.9 us (3%)
  between operations  39.5 us (3%)
    ppermute x38, starting transfers between devices, swap(): lax.ppermute(value, 'row', [(s, s ^ distance) for s in range(row_count)])  416 us
    ppermute x38, waiting for transfers between devices, swap(): lax.ppermute(value, 'row', [(s, s ^ distance) for s in range(row_count)])  365 us
    all_gather x1, waiting for transfers between devices, body(): candidates = lax.all_gather(reflectors, 'col', axis=0)  196 us
    psum x1, waiting for transfers between devices, body(): lax.psum(jnp.concatenate([partial_value, told], axis=0), 'row')  86.7 us
    pallas_call x4, Pallas kernels, settle_there(): pl.pallas_call(functools.partial(settle_kernel, groups, count), grid_spec...  64.1 us
    pallas_call x4, Pallas kernels, finish_here(): pl.pallas_call(functools.partial(finish_kernel, groups, count), grid_spec...  63.4 us
    dot_general x2, matrix products, body(): lax.dot_general(panel, eigvecs, contract_rows, preferred_element_type=jnp...  35.2 us
  transfers between devices with their start and end apart: 42, of which 11 were waited for; matrix products, arithmetic and copies ran while one was open for 9% of the time, Pallas kernels for 11%

profile of v5, /device:TPU:0, one launch (start us, length us, event | category | flops | bytes accessed | tf_op | source)
XLA Modules:
  0.0 1401.4 jit_solution(476657121151224486)
XLA Ops:
  17.1 196.1 %all-gather.5.cloned.1.call-done = bf16[65536,256]{1,0:T(8,128)(2,1)} async-done(((bf16[16384,256]{1,0:T(8,128)(2,1)}), bf16[65536,256]{1,0:T(8,128)(2,1)}) %all-gather.5.cloned.1.call-update) | async-done | bytes 33554448 | tf_op jit(solution)/shard_map/all_gather | solution.py:318
  228.0 17.7 %convolution_convert_fusion.2 = bf16[256,1024]{1,0:T(8,128)(2,1)S(1)} fusion(bf16[16384,1024]{1,0:T(8,128)(2,1)} %param.8, bf16[1,16384,256]{2,1,0:T(8,128)(2,1)} %copy-done.1), kind=kOutput, calls=%fused_computation.26 | convolution fusion | flops 8590196736 | bytes 42467328 | tf_op jit(solution)/shard_map/dot_general | solution.py:325
  245.7 17.5 %convolution_convert_fusion.3 = bf16[256,1024]{1,0:T(8,128)(2,1)S(1)} fusion(bf16[16384,1024]{1,0:T(8,128)(2,1)} %param.8, bf16[1,16384,256]{2,1,0:T(8,128)(2,1)} %copy-done), kind=kOutput, calls=%fused_computation.27 | convolution fusion | flops 8590196736 | bytes 42467328 | tf_op jit(solution)/shard_map/dot_general | solution.py:325
  283.3 86.7 %all-reduce.5.cloned.1.call-done = bf16[528,1280]{1,0:T(8,128)(2,1)} async-done(((bf16[528,1280]{1,0:T(8,128)(2,1)}), bf16[528,1280]{1,0:T(8,128)(2,1)}) %all-reduce.5.cloned.1.call-update) | async-done | bytes 1351696 | tf_op jit(solution)/shard_map/psum | solution.py:335
  380.7 11.0 shard_map.68
  404.1 11.1 collective-permute-start.5
  417.0 8.3 shard_map.73
  436.6 194.4 %collective-permute-done.17.refs_0_ = bf16[1,128,1024]{2,1,0:T(8,128)(2,1)} collective-permute-done((bf16[1,128,1024]{2,1,0:T(8,128)(2,1)}, bf16[1,128,1024]{2,1,0:T(8,128)(2,1)}, u32[]{:S(2)}, u32[]{:S(2)}) %collective-permute-start.17) | collective-permute-done | bytes 262176 | tf_op jit(solution)/shard_map/ppermute | solution.py:16
  634.2 8.3 collective-permute-done.18.refs_1_
  648.5 7.9 shard_map.70
  660.5 87.1 %collective-permute-start.15 = (bf16[11,128,1024]{2,1,0:T(8,128)(2,1)}, bf16[11,128,1024]{2,1,0:T(8,128)(2,1)}, u32[]{:S(2)}, u32[]{:S(2)}) collective-permute-start(bf16[11,128,1024]{2,1,0:T(8,128)(2,1)} %get-tuple-element.100), channel_id=1, source_target_pairs={{0,8},{4,12},{8,0},{12,4},{16,24},{20,28},{24,16},{28,20},{1,9},{5... | collective-permute-start | bytes 8650760 | tf_op jit(solution)/shard_map/ppermute | solution.py:16
  751.4 19.8 %shard_map.75 = (bf16[8,128,1024]{2,1,0:T(8,128)(2,1)}, bf16[8,128,1024]{2,1,0:T(8,128)(2,1)}, bf16[8,128,1024]{2,1,0:T(8,128)(2,1)}) custom-call(s32[24]{0:T(128)} %get-tuple-element.232.block_ref, s32[24]{0:T(128)} %get-tuple-element.231.filled_ref, s32[1]{0:T(128)} %constant.200.clone.1.base_ref, bf16[128,128,1024]{2,1,0:T(8,128)(2,1)} %bitcast.159, ...), custom_call_target="tpu_custom_call" | custom-call | tf_op jit(solution)/shard_map/pallas_call | solution.py:103
  771.4 89.0 %collective-permute-start.26 = (bf16[8,128,1024]{2,1,0:T(8,128)(2,1)}, bf16[8,128,1024]{2,1,0:T(8,128)(2,1)}, u32[]{:S(2)}, u32[]{:S(2)}) collective-permute-start(bf16[8,128,1024]{2,1,0:T(8,128)(2,1)} %get-tuple-element.111), channel_id=1, source_target_pairs={{0,8},{4,12},{8,0},{12,4},{16,24},{20,28},{24,16},{28,20},{1,9},{5... | collective-permute-start | bytes 6291464 | tf_op jit(solution)/shard_map/ppermute | solution.py:16
  861.7 50.8 %collective-permute-start.27 = (bf16[8,128,1024]{2,1,0:T(8,128)(2,1)}, bf16[8,128,1024]{2,1,0:T(8,128)(2,1)}, u32[]{:S(2)}, u32[]{:S(2)}) collective-permute-start(bf16[8,128,1024]{2,1,0:T(8,128)(2,1)} %get-tuple-element.112), channel_id=1, source_target_pairs={{0,12},{4,8},{8,4},{12,0},{16,28},{20,24},{24,20},{28,16},{1,13},{... | collective-permute-start | bytes 6291464 | tf_op jit(solution)/shard_map/ppermute | solution.py:16
  914.1 18.2 %shard_map.76 = (bf16[6,128,1024]{2,1,0:T(8,128)(2,1)}, bf16[6,128,1024]{2,1,0:T(8,128)(2,1)}, bf16[6,128,1024]{2,1,0:T(8,128)(2,1)}, bf16[6,128,1024]{2,1,0:T(8,128)(2,1)}) custom-call(s32[24]{0:T(128)} %get-tuple-element.230.block_ref, s32[24]{0:T(128)} %get-tuple-element.229.filled_ref, s32[1]{0:T(128)} %constant.200.clone.1.base_ref, ...), custom_call_target="tpu_custom_call" | custom-call | tf_op jit(solution)/shard_map/pallas_call | solution.py:103
  945.2 14.3 %shard_map.64.owned_ref = bf16[160,128,1024]{2,1,0:T(8,128)(2,1)} custom-call(s32[20]{0:T(128)} %get-tuple-element.246.block_ref, s32[20]{0:T(128)} %get-tuple-element.245.filled_ref, s32[1]{0:T(128)} %bitcast.41.base_ref, bf16[128,128,1024]{2,1,0:T(8,128)(2,1)} %bitcast.161, bf16[128,128,256]{2,1,0:T(8,128)(2,1)} %bitcast.167, ...), custom_call_target="tpu_custom_call" | custom-call | tf_op jit(solution)/shard_map/pallas_call | solution.py:103
  964.6 27.7 %shard_map.71.owned_ref = bf16[160,128,1024]{2,1,0:T(8,128)(2,1)} custom-call(s32[33]{0:T(128)} %pad_add_fusion.12.slot_ref, bf16[160,128,1024]{2,1,0:T(8,128)(2,1)} %shard_map.69.owned_ref, bf16[11,128,1024]{2,1,0:T(8,128)(2,1)} %collective-permute-done.14.refs_0_, ...), custom_call_target="tpu_custom_call", output_to_operand_aliasing={{}: (1, {})} | custom-call | tf_op jit(solution)/shard_map/pallas_call | solution.py:142
  997.4 26.9 %shard_map.74 = bf16[160,128,1024]{2,1,0:T(8,128)(2,1)} custom-call(s32[32]{0:T(128)} %pad_add_fusion.10.slot_ref, bf16[160,128,1024]{2,1,0:T(8,128)(2,1)} %shard_map.72.owned_ref, bf16[8,128,1024]{2,1,0:T(8,128)(2,1)} %copy-done.5, bf16[8,128,1024]{2,1,0:T(8,128)(2,1)} %collective-permute-done.22.refs_1_, ...), custom_call_target="tpu_custom_call", output_to_operand_aliasing={{}: (1, {})} | custom-call | tf_op jit(solution)/shard_map/pallas_call | solution.py:142
  1030.5 62.6 %collective-permute-start.32 = (bf16[3,128,1024]{2,1,0:T(8,128)(2,1)}, bf16[3,128,1024]{2,1,0:T(8,128)(2,1)}, u32[]{:S(2)}, u32[]{:S(2)}) collective-permute-start(bf16[3,128,1024]{2,1,0:T(8,128)(2,1)} %get-tuple-element.88), channel_id=1, source_target_pairs={{0,16},{4,20},{8,24},{12,28},{16,0},{20,4},{24,8},{28,12},{1,17},{... | collective-permute-start | bytes 2359304 | tf_op jit(solution)/shard_map/ppermute | solution.py:16
  1099.3 58.2 %collective-permute-done.29.rest_1_ = bf16[6,128,1024]{2,1,0:T(8,128)(2,1)} collective-permute-done((bf16[6,128,1024]{2,1,0:T(8,128)(2,1)}, bf16[6,128,1024]{2,1,0:T(8,128)(2,1)}, u32[]{:S(2)}, u32[]{:S(2)}) %collective-permute-start.29) | collective-permute-done | bytes 1572896 | tf_op jit(solution)/shard_map/ppermute | solution.py:16
  1169.5 65.1 %collective-permute-start.33 = (bf16[3,128,1024]{2,1,0:T(8,128)(2,1)}, bf16[3,128,1024]{2,1,0:T(8,128)(2,1)}, u32[]{:S(2)}, u32[]{:S(2)}) collective-permute-start(bf16[3,128,1024]{2,1,0:T(8,128)(2,1)} %get-tuple-element.89), channel_id=1, source_target_pairs={{0,20},{4,16},{8,28},{12,24},{16,4},{20,0},{24,12},{28,8},{1,21},{... | collective-permute-start | bytes 2359304 | tf_op jit(solution)/shard_map/ppermute | solution.py:16
  1242.9 32.7 %collective-permute-done.32 = bf16[3,128,1024]{2,1,0:T(8,128)(2,1)} collective-permute-done((bf16[3,128,1024]{2,1,0:T(8,128)(2,1)}, bf16[3,128,1024]{2,1,0:T(8,128)(2,1)}, u32[]{:S(2)}, u32[]{:S(2)}) %collective-permute-start.32) | collective-permute-done | bytes 786464 | tf_op jit(solution)/shard_map/ppermute | solution.py:16
  1277.3 15.0 %collective-permute-done.33 = bf16[3,128,1024]{2,1,0:T(8,128)(2,1)} collective-permute-done((bf16[3,128,1024]{2,1,0:T(8,128)(2,1)}, bf16[3,128,1024]{2,1,0:T(8,128)(2,1)}, u32[]{:S(2)}, u32[]{:S(2)}) %collective-permute-start.33) | collective-permute-done | bytes 786464 | tf_op jit(solution)/shard_map/ppermute | solution.py:16
  1324.6 44.0 %collective-permute-done.35 = bf16[3,128,1024]{2,1,0:T(8,128)(2,1)} collective-permute-done((bf16[3,128,1024]{2,1,0:T(8,128)(2,1)}, bf16[3,128,1024]{2,1,0:T(8,128)(2,1)}, u32[]{:S(2)}, u32[]{:S(2)}) %collective-permute-start.35) | collective-permute-done | bytes 786464 | tf_op jit(solution)/shard_map/ppermute | solution.py:16
  (311 shorter events, 195.0 us)
Async XLA Ops:
  6.5 206.6 %all-gather.5.cloned.1.call-start = ((), (), s32[]{:S(2)}) async-start(), calls=%async_computation.2 | async-start | bytes 41943040 | tf_op jit(solution)/shard_map/all_gather | solution.py:318
  7.3 276.0 %all-reduce.7.cloned.1.call-start = ((), (), s32[]{:S(2)}) async-start(), calls=%async_computation.1 | async-start | bytes 1048576 | tf_op jit(solution)/shard_map/psum | solution.py:321
  10.1 359.8 %all-reduce.5.cloned.1.call-start = ((), (), s32[]{:S(2)}) async-start(), calls=%async_computation | async-start | bytes 2703360 | tf_op jit(solution)/shard_map/psum | solution.py:335
  264.4 695.9 %all-gather.7.cloned.1.call-start = ((), (), s32[]{:S(2)}) async-start(), calls=%async_computation.3 | async-start | bytes 11796480 | tf_op jit(solution)/shard_map/all_gather | solution.py:372
  425.3 235.2 %collective-permute-start.21 = (bf16[8,128,1024]{2,1,0:T(8,128)(2,1)}, bf16[8,128,1024]{2,1,0:T(8,128)(2,1)S(1)}, u32[]{:S(2)}, u32[]{:S(2)}) collective-permute-start(bf16[8,128,1024]{2,1,0:T(8,128)(2,1)} %get-tuple-element.106), channel_id=1, source_target_pairs={{0,16},{4,20},{8,24},{12,28},{16,0},{20,4},{24,8},{28,12},{1,17},{... | collective-permute-start | bytes 6291464 | tf_op jit(solution)/shard_map/ppermute | solution.py:16
  428.1 321.3 %collective-permute-start.22 = (bf16[8,128,1024]{2,1,0:T(8,128)(2,1)}, bf16[8,128,1024]{2,1,0:T(8,128)(2,1)}, u32[]{:S(2)}, u32[]{:S(2)}) collective-permute-start(bf16[8,128,1024]{2,1,0:T(8,128)(2,1)} %get-tuple-element.107), channel_id=1, source_target_pairs={{0,20},{4,16},{8,28},{12,24},{16,4},{20,0},{24,12},{28,8},{1,21},{... | collective-permute-start | bytes 6291464 | tf_op jit(solution)/shard_map/ppermute | solution.py:16
  430.0 201.0 %collective-permute-start.17 = (bf16[1,128,1024]{2,1,0:T(8,128)(2,1)}, bf16[1,128,1024]{2,1,0:T(8,128)(2,1)}, u32[]{:S(2)}, u32[]{:S(2)}) collective-permute-start(bf16[1,128,1024]{2,1,0:T(8,128)(2,1)} %get-tuple-element.102), channel_id=1, source_target_pairs={{0,16},{4,20},{8,24},{12,28},{16,0},{20,4},{24,8},{28,12},{1,17},{... | collective-permute-start | bytes 786440 | tf_op jit(solution)/shard_map/ppermute | solution.py:16
  432.6 210.0 %collective-permute-start.18 = (bf16[1,128,1024]{2,1,0:T(8,128)(2,1)}, bf16[1,128,1024]{2,1,0:T(8,128)(2,1)}, u32[]{:S(2)}, u32[]{:S(2)}) collective-permute-start(bf16[1,128,1024]{2,1,0:T(8,128)(2,1)} %get-tuple-element.103), channel_id=1, source_target_pairs={{0,20},{4,16},{8,28},{12,24},{16,4},{20,0},{24,12},{28,8},{1,21},{... | collective-permute-start | bytes 786440 | tf_op jit(solution)/shard_map/ppermute | solution.py:16
  433.3 223.1 %collective-permute-start.19 = (bf16[1,128,1024]{2,1,0:T(8,128)(2,1)}, bf16[1,128,1024]{2,1,0:T(8,128)(2,1)}, u32[]{:S(2)}, u32[]{:S(2)}) collective-permute-start(bf16[1,128,1024]{2,1,0:T(8,128)(2,1)} %get-tuple-element.104), channel_id=1, source_target_pairs={{0,24},{4,28},{8,16},{12,20},{16,8},{20,12},{24,0},{28,4},{1,25},{... | collective-permute-start | bytes 786440 | tf_op jit(solution)/shard_map/ppermute | solution.py:16
  642.5 128.7 %collective-permute-start.23 = (bf16[8,128,1024]{2,1,0:T(8,128)(2,1)}, bf16[8,128,1024]{2,1,0:T(8,128)(2,1)}, u32[]{:S(2)}, u32[]{:S(2)}) collective-permute-start(bf16[8,128,1024]{2,1,0:T(8,128)(2,1)} %get-tuple-element.108), channel_id=1, source_target_pairs={{0,24},{4,28},{8,16},{12,20},{16,8},{20,12},{24,0},{28,4},{1,25},{... | collective-permute-start | bytes 6291464 | tf_op jit(solution)/shard_map/ppermute | solution.py:16
  656.4 205.3 %collective-permute-start.14 = (bf16[11,128,1024]{2,1,0:T(8,128)(2,1)}, bf16[11,128,1024]{2,1,0:T(8,128)(2,1)}, u32[]{:S(2)}, u32[]{:S(2)}) collective-permute-start(bf16[11,128,1024]{2,1,0:T(8,128)(2,1)} %get-tuple-element.99), channel_id=1, source_target_pairs={{0,4},{4,0},{8,12},{12,8},{16,20},{20,16},{24,28},{28,24},{1,5},{5... | collective-permute-start | bytes 8650760 | tf_op jit(solution)/shard_map/ppermute | solution.py:16
  660.5 273.1 %collective-permute-start.15 = (bf16[11,128,1024]{2,1,0:T(8,128)(2,1)}, bf16[11,128,1024]{2,1,0:T(8,128)(2,1)}, u32[]{:S(2)}, u32[]{:S(2)}) collective-permute-start(bf16[11,128,1024]{2,1,0:T(8,128)(2,1)} %get-tuple-element.100), channel_id=1, source_target_pairs={{0,8},{4,12},{8,0},{12,4},{16,24},{20,28},{24,16},{28,20},{1,9},{5... | collective-permute-start | bytes 8650760 | tf_op jit(solution)/shard_map/ppermute | solution.py:16
  749.3 187.7 %collective-permute-start.16 = (bf16[11,128,1024]{2,1,0:T(8,128)(2,1)}, bf16[11,128,1024]{2,1,0:T(8,128)(2,1)}, u32[]{:S(2)}, u32[]{:S(2)}) collective-permute-start(bf16[11,128,1024]{2,1,0:T(8,128)(2,1)} %get-tuple-element.101), channel_id=1, source_target_pairs={{0,12},{4,8},{8,4},{12,0},{16,28},{20,24},{24,20},{28,16},{1,13},{... | collective-permute-start | bytes 8650760 | tf_op jit(solution)/shard_map/ppermute | solution.py:16
  771.2 167.1 %collective-permute-start.25 = (bf16[8,128,1024]{2,1,0:T(8,128)(2,1)}, bf16[8,128,1024]{2,1,0:T(8,128)(2,1)S(1)}, u32[]{:S(2)}, u32[]{:S(2)}) collective-permute-start(bf16[8,128,1024]{2,1,0:T(8,128)(2,1)} %get-tuple-element.110), channel_id=1, source_target_pairs={{0,4},{4,0},{8,12},{12,8},{16,20},{20,16},{24,28},{28,24},{1,5},{5... | collective-permute-start | bytes 6291464 | tf_op jit(solution)/shard_map/ppermute | solution.py:16
  771.4 172.9 %collective-permute-start.26 = (bf16[8,128,1024]{2,1,0:T(8,128)(2,1)}, bf16[8,128,1024]{2,1,0:T(8,128)(2,1)}, u32[]{:S(2)}, u32[]{:S(2)}) collective-permute-start(bf16[8,128,1024]{2,1,0:T(8,128)(2,1)} %get-tuple-element.111), channel_id=1, source_target_pairs={{0,8},{4,12},{8,0},{12,4},{16,24},{20,28},{24,16},{28,20},{1,9},{5... | collective-permute-start | bytes 6291464 | tf_op jit(solution)/shard_map/ppermute | solution.py:16
  861.7 168.8 %collective-permute-start.27 = (bf16[8,128,1024]{2,1,0:T(8,128)(2,1)}, bf16[8,128,1024]{2,1,0:T(8,128)(2,1)}, u32[]{:S(2)}, u32[]{:S(2)}) collective-permute-start(bf16[8,128,1024]{2,1,0:T(8,128)(2,1)} %get-tuple-element.112), channel_id=1, source_target_pairs={{0,12},{4,8},{8,4},{12,0},{16,28},{20,24},{24,20},{28,16},{1,13},{... | collective-permute-start | bytes 6291464 | tf_op jit(solution)/shard_map/ppermute | solution.py:16
  933.6 162.5 %collective-permute-start.28 = (bf16[6,128,1024]{2,1,0:T(8,128)(2,1)}, bf16[6,128,1024]{2,1,0:T(8,128)(2,1)}, u32[]{:S(2)}, u32[]{:S(2)}) collective-permute-start(bf16[6,128,1024]{2,1,0:T(8,128)(2,1)} %get-tuple-element.113), channel_id=1, source_target_pairs={{0,16},{4,20},{8,24},{12,28},{16,0},{20,4},{24,8},{28,12},{1,17},{... | collective-permute-start | bytes 4718600 | tf_op jit(solution)/shard_map/ppermute | solution.py:16
  937.0 220.4 %collective-permute-start.29 = (bf16[6,128,1024]{2,1,0:T(8,128)(2,1)}, bf16[6,128,1024]{2,1,0:T(8,128)(2,1)}, u32[]{:S(2)}, u32[]{:S(2)}) collective-permute-start(bf16[6,128,1024]{2,1,0:T(8,128)(2,1)} %get-tuple-element.114), channel_id=1, source_target_pairs={{0,20},{4,16},{8,28},{12,24},{16,4},{20,0},{24,12},{28,8},{1,21},{... | collective-permute-start | bytes 4718600 | tf_op jit(solution)/shard_map/ppermute | solution.py:16
  938.3 222.2 %collective-permute-start.30 = (bf16[6,128,1024]{2,1,0:T(8,128)(2,1)}, bf16[6,128,1024]{2,1,0:T(8,128)(2,1)}, u32[]{:S(2)}, u32[]{:S(2)}) collective-permute-start(bf16[6,128,1024]{2,1,0:T(8,128)(2,1)} %get-tuple-element.115), channel_id=1, source_target_pairs={{0,24},{4,28},{8,16},{12,20},{16,8},{20,12},{24,0},{28,4},{1,25},{... | collective-permute-start | bytes 4718600 | tf_op jit(solution)/shard_map/ppermute | solution.py:16
  944.3 219.3 %collective-permute-start.31 = (bf16[6,128,1024]{2,1,0:T(8,128)(2,1)}, bf16[6,128,1024]{2,1,0:T(8,128)(2,1)S(1)}, u32[]{:S(2)}, u32[]{:S(2)}) collective-permute-start(bf16[6,128,1024]{2,1,0:T(8,128)(2,1)} %get-tuple-element.116), channel_id=1, source_target_pairs={{0,28},{4,24},{8,20},{12,16},{16,12},{20,8},{24,4},{28,0},{1,29},{... | collective-permute-start | bytes 4718600 | tf_op jit(solution)/shard_map/ppermute | solution.py:16
  1030.5 245.1 %collective-permute-start.32 = (bf16[3,128,1024]{2,1,0:T(8,128)(2,1)}, bf16[3,128,1024]{2,1,0:T(8,128)(2,1)}, u32[]{:S(2)}, u32[]{:S(2)}) collective-permute-start(bf16[3,128,1024]{2,1,0:T(8,128)(2,1)} %get-tuple-element.88), channel_id=1, source_target_pairs={{0,16},{4,20},{8,24},{12,28},{16,0},{20,4},{24,8},{28,12},{1,17},{... | collective-permute-start | bytes 2359304 | tf_op jit(solution)/shard_map/ppermute | solution.py:16
  1169.5 122.8 %collective-permute-start.33 = (bf16[3,128,1024]{2,1,0:T(8,128)(2,1)}, bf16[3,128,1024]{2,1,0:T(8,128)(2,1)}, u32[]{:S(2)}, u32[]{:S(2)}) collective-permute-start(bf16[3,128,1024]{2,1,0:T(8,128)(2,1)} %get-tuple-element.89), channel_id=1, source_target_pairs={{0,20},{4,16},{8,28},{12,24},{16,4},{20,0},{24,12},{28,8},{1,21},{... | collective-permute-start | bytes 2359304 | tf_op jit(solution)/shard_map/ppermute | solution.py:16
  1242.5 148.4 %collective-permute-start.36 = (bf16[6,128,1024]{2,1,0:T(8,128)(2,1)}, bf16[6,128,1024]{2,1,0:T(8,128)(2,1)S(1)}, u32[]{:S(2)}, u32[]{:S(2)}) collective-permute-start(bf16[6,128,1024]{2,1,0:T(8,128)(2,1)} %get-tuple-element.118), channel_id=1, source_target_pairs={{0,4},{4,0},{8,12},{12,8},{16,20},{20,16},{24,28},{28,24},{1,5},{5... | collective-permute-start | bytes 4718600 | tf_op jit(solution)/shard_map/ppermute | solution.py:16
  1242.9 148.0 %collective-permute-start.37 = (bf16[6,128,1024]{2,1,0:T(8,128)(2,1)}, bf16[6,128,1024]{2,1,0:T(8,128)(2,1)S(1)}, u32[]{:S(2)}, u32[]{:S(2)}) collective-permute-start(bf16[6,128,1024]{2,1,0:T(8,128)(2,1)} %get-tuple-element.119), channel_id=1, source_target_pairs={{0,8},{4,12},{8,0},{12,4},{16,24},{20,28},{24,16},{28,20},{1,9},{5... | collective-permute-start | bytes 4718600 | tf_op jit(solution)/shard_map/ppermute | solution.py:16
  (60 other events, 2510.6 us)
Sparse Core Ops, SparseCore 0:
  8.9 204.2 all-gather.4
  215.5 33.3 all-reduce.6
  264.5 105.4 all-reduce.4
  399.7 72.5 all-gather.6
